TPU v7x, 32 devices: a whole 2x2x4 slice. The times are simulated.
32 devices in a mesh: seq: 16 (over z, y, core), head: 2 (over x).
Axes of the slice: x: 2, y: 2, z: 4, core: 2. Of those that a mesh axis runs over, the one named last changes fastest.
Arguments:
- tokens: bfloat16 [512, 2048], P('seq', 'head'), may hold values from -6 to 6
- ln1_gain: float32 [2048], replicated, may hold values from 0.1 to 1.9
- ln1_shift: float32 [2048], replicated, may hold values from -1.75 to 1.75
- ln2_gain: float32 [2048], replicated, may hold values from 0.1 to 1.9
- ln2_shift: float32 [2048], replicated, may hold values from -1.75 to 1.75
- w_qkv: bfloat16 [2048, 3, 2048], P(None, None, 'head'), may hold values from -0.125 to 0.125
- b_qkv: float32 [3, 2048], P(None, 'head'), may hold values from -3 to 3
- w_dense: bfloat16 [2048, 2048], P('head'), may hold values from -0.125 to 0.125
- b_dense: float32 [2048], P('head'), may hold values from -1.75 to 1.75
- w_up: bfloat16 [2048, 4096], P(None, 'head'), may hold values from -0.125 to 0.125
- b_up: float32 [4096], P('head'), may hold values from -3 to 3
- w_down: bfloat16 [4096, 2048], P('head'), may hold values from -0.09375 to 0.09375
- b_down: float32 [2048], P('head'), may hold values from -1.75 to 1.75
- keys_short: bfloat16 [512, 64, 2048], P('seq', None, 'head'), may hold values from -210 to 210
- values_short: bfloat16 [512, 64, 2048], P('seq', None, 'head'), may hold values from -16 to 16
- keys_long: bfloat16 [32768, 2048], P('seq', 'head'), may hold values from -210 to 210
- values_long: bfloat16 [32768, 2048], P('seq', 'head'), may hold values from -16 to 16
- lengths: int32 [512], replicated, may hold values from 16 to 8192, as said below
- slot_request: int32 [512], replicated, may hold values from 0 to 511, as said below
- piece_map: int32 [16], replicated, may hold values from 0 to 15, each once
Outputs:
- layer_out: bfloat16 [512, 2048], P('seq', 'head')
Inputs may be any that keep to these rules, and one draw needn't show every extreme that they name: `lengths`: requests 0 to 3 hold more than 4096 positions, one of them exactly 8192; every other request holds 16 to 64 positions, one of them exactly 64. `slot_request`: A permutation of the requests; slot s lies on index s // 32 of seq. The requests 32 h to 32 h + 31 are served in 8 groups of exactly 4 on as many different indices of seq. Rows 2048 b to 2048 b + 2047 of keys_long and values_long hold positions (piece_map[b] % 4) * 2048 onwards of the cache of request piece_map[b] // 4.
All inputs are finite; a program needn't handle non-finite values.
Results may differ from a plain program's by a relative error of at most 0.0095.
Values may be sent and summed in bfloat16 or wider, within the bound.
A program may use at most 192 MiB of HBM per device.

v0:
```python
import jax
import jax.numpy as jnp
from jax import lax
from jax.sharding import PartitionSpec as P

HD = 256
ROT = 64
LONGS = 4


epsilon = 1e-05
very_low = -1e30


def merged(array, axis, combine):
    everything = jax.tree.map(lambda part: lax.all_gather(part, axis), array)
    first = jax.tree.map(lambda part: part[0], everything)

    def hop(k, so_far):
        return combine(so_far, jax.tree.map(lambda part: part[k], everything))

    return lax.fori_loop(1, lax.axis_size(axis), hop, first)


def layer_norm(values, gain, shift):
    center = jnp.mean(values, axis=-1, keepdims=True)
    offset = values - center
    spread = jnp.mean(offset * offset, axis=-1, keepdims=True)
    return offset * lax.rsqrt(spread + epsilon) * gain + shift


def rotary(values, position):
    half_rot = ROT // 2
    frequency = jnp.power(10000.0, -2.0 * jnp.arange(half_rot, dtype=jnp.float32) / ROT)
    angles = position.astype(jnp.float32)[:, None] * frequency[None, :]
    cosine = jnp.cos(angles)[:, None, :]
    sine_of = jnp.sin(angles)[:, None, :]
    leading = values[..., :half_rot]
    trailing = values[..., half_rot:ROT]
    return jnp.concatenate(
        [
            leading * cosine - trailing * sine_of,
            trailing * cosine + leading * sine_of,
            values[..., ROT:],
        ],
        axis=-1,
    )


def attend(queries, key_rows, value_rows, usable):
    scores = jnp.einsum(
        "rhc,rthc->rht", queries, key_rows, preferred_element_type=jnp.float32
    ) * HD ** (-0.5)
    masked = jnp.where(usable[:, None, :], scores, very_low)
    summit = jnp.max(masked, axis=-1)
    weights = jnp.where(usable[:, None, :], jnp.exp(masked - summit[..., None]), 0.0)
    amount = jnp.sum(weights, axis=-1)
    mixed = jnp.einsum(
        "rht,rthc->rhc",
        weights.astype(jnp.bfloat16),
        value_rows,
        preferred_element_type=jnp.float32,
    )
    return (summit, amount, mixed)


def combine_partials(first_part, second_part):
    top_first, total_first, out_first = first_part
    top_second, total_second, out_second = second_part
    summit = jnp.maximum(top_first, top_second)
    scale_first = jnp.exp(top_first - summit)
    scale_second = jnp.exp(top_second - summit)
    total_both = total_first * scale_first + total_second * scale_second
    out_both = out_first * scale_first[..., None] + out_second * scale_second[..., None]
    return (summit, total_both, out_both)


def local(
    tokens,
    ln1_gain,
    ln1_shift,
    ln2_gain,
    ln2_shift,
    w_qkv,
    b_qkv,
    w_dense,
    b_dense,
    w_up,
    b_up,
    w_down,
    b_down,
    keys_short,
    values_short,
    keys_long,
    values_long,
    lengths,
    slot_request,
    piece_map,
):
    slot_rows, part_width = tokens.shape
    seq_count = lax.axis_size("seq")
    seq_place = lax.axis_index("seq")
    request_count = slot_request.shape[0]
    heads_here = part_width // HD
    my_requests = lax.dynamic_slice_in_dim(slot_request, seq_place * slot_rows, slot_rows)
    shard_rows = lax.all_gather(tokens, "seq", axis=0, tiled=True)
    row_ids = jnp.arange(shard_rows.shape[0], dtype=jnp.int32)
    selector = (my_requests[:, None] == row_ids[None, :]).astype(jnp.bfloat16)
    own_cols = jnp.dot(selector, shard_rows, preferred_element_type=jnp.float32).astype(
        jnp.bfloat16
    )
    full_rows = lax.all_gather(own_cols, "head", axis=1, tiled=True)
    resident = full_rows.astype(jnp.float32)
    normed_attn = layer_norm(resident, ln1_gain, ln1_shift).astype(jnp.bfloat16)
    normed_mlp = layer_norm(resident, ln2_gain, ln2_shift).astype(jnp.bfloat16)
    projected = jnp.dot(
        normed_attn,
        w_qkv.reshape(w_qkv.shape[0], 3 * part_width),
        preferred_element_type=jnp.float32,
    )
    projected = projected.reshape(slot_rows, 3, part_width) + b_qkv[None]
    request_ids = jnp.arange(request_count, dtype=jnp.int32)
    my_lengths = jnp.sum(
        jnp.where(my_requests[:, None] == request_ids[None, :], lengths[None, :], 0), axis=1
    )
    queries = rotary(projected[:, 0].reshape(slot_rows, heads_here, HD), my_lengths).astype(
        jnp.bfloat16
    )
    new_keys = rotary(projected[:, 1].reshape(slot_rows, heads_here, HD), my_lengths).astype(
        jnp.bfloat16
    )
    new_values = projected[:, 2].reshape(slot_rows, heads_here, HD).astype(jnp.bfloat16)
    long_hits = my_requests[:, None] == jnp.arange(LONGS, dtype=jnp.int32)[None, :]
    long_part = jnp.sum(
        jnp.where(long_hits[:, :, None, None], queries.astype(jnp.float32)[:, None], 0.0), axis=0
    )
    long_queries = lax.psum(long_part, "seq")
    short_max = keys_short.shape[1]
    short_usable = (jnp.arange(short_max, dtype=jnp.int32)[None, :] < my_lengths[:, None]) & (
        my_lengths <= short_max
    )[:, None]
    short_keys = keys_short.reshape(slot_rows, short_max, heads_here, HD)
    short_vals = values_short.reshape(slot_rows, short_max, heads_here, HD)
    short_top, short_total, short_out = attend(queries, short_keys, short_vals, short_usable)
    own_score = jnp.sum(
        queries.astype(jnp.float32) * new_keys.astype(jnp.float32), axis=-1
    ) * HD ** (-0.5)
    piece_count = seq_count // LONGS
    my_piece = lax.dynamic_slice_in_dim(piece_map, seq_place, 1)[0]
    long_owner = my_piece // piece_count
    piece_index = my_piece % piece_count
    long_pick = jnp.arange(LONGS, dtype=jnp.int32) == long_owner
    piece_query = jnp.sum(jnp.where(long_pick[:, None, None], long_queries, 0.0), axis=0).astype(
        jnp.bfloat16
    )
    long_length = jnp.sum(jnp.where(long_pick, lengths[:LONGS], 0))
    piece_len = keys_long.shape[0]
    positions = piece_index * piece_len + jnp.arange(piece_len, dtype=jnp.int32)
    piece_usable = (positions < long_length)[None, :]
    piece_keys = keys_long.reshape(1, piece_len, heads_here, HD)
    piece_vals = values_long.reshape(1, piece_len, heads_here, HD)
    piece_top, piece_total, piece_out = attend(
        piece_query[None], piece_keys, piece_vals, piece_usable
    )
    spread_top = jnp.where(long_pick[:, None], piece_top, very_low)
    spread_total = jnp.where(long_pick[:, None], piece_total, 0.0)
    spread_out = jnp.where(long_pick[:, None, None], piece_out, 0.0)
    long_top, long_total, long_out = merged(
        (spread_top, spread_total, spread_out), "seq", combine_partials
    )
    has_long = jnp.any(long_hits, axis=1)
    mine_top = jnp.where(
        has_long[:, None],
        jnp.sum(jnp.where(long_hits[:, :, None], long_top[None], 0.0), axis=1),
        very_low,
    )
    mine_total = jnp.sum(jnp.where(long_hits[:, :, None], long_total[None], 0.0), axis=1)
    mine_out = jnp.sum(jnp.where(long_hits[:, :, None, None], long_out[None], 0.0), axis=1)
    summit = jnp.maximum(jnp.maximum(short_top, own_score), mine_top)
    short_scale = jnp.exp(short_top - summit)
    own_scale = jnp.exp(own_score - summit)
    long_scale = jnp.exp(mine_top - summit)
    denominator = short_total * short_scale + own_scale + mine_total * long_scale
    numerator = (
        short_out * short_scale[..., None]
        + new_values.astype(jnp.float32) * own_scale[..., None]
        + mine_out * long_scale[..., None]
    )
    attended = (
        (numerator / denominator[..., None]).reshape(slot_rows, part_width).astype(jnp.bfloat16)
    )
    hidden_units = jax.nn.gelu(
        jnp.dot(normed_mlp, w_up, preferred_element_type=jnp.float32) + b_up, approximate=False
    ).astype(jnp.bfloat16)
    partial_sum = jnp.dot(attended, w_dense, preferred_element_type=jnp.float32) + jnp.dot(
        hidden_units, w_down, preferred_element_type=jnp.float32
    )
    head_total = lax.psum_scatter(
        partial_sum.astype(jnp.bfloat16), "head", scatter_dimension=1, tiled=True
    ).astype(jnp.float32)
    finished = (own_cols.astype(jnp.float32) + head_total + b_dense + b_down).astype(jnp.bfloat16)
    home_ids = seq_place * slot_rows + jnp.arange(slot_rows, dtype=jnp.int32)
    selector = (slot_request[None, :] == home_ids[:, None]).astype(jnp.bfloat16)
    return jnp.dot(
        selector,
        lax.all_gather(finished, "seq", axis=0, tiled=True),
        preferred_element_type=jnp.float32,
    ).astype(jnp.bfloat16)


def solution(mesh):
    in_specs = (
        P("seq", "head"),
        P(),
        P(),
        P(),
        P(),
        P(None, None, "head"),
        P(None, "head"),
        P("head", None),
        P("head"),
        P(None, "head"),
        P("head"),
        P("head", None),
        P("head"),
        P("seq", None, "head"),
        P("seq", None, "head"),
        P("seq", "head"),
        P("seq", "head"),
        P(),
        P(),
        P(),
    )
    out_specs = P("seq", "head")
    return jax.shard_map(local, mesh=mesh, in_specs=in_specs, out_specs=out_specs, check_vma=False)
```

profile of v0, /device:TPU:0, one launch (start us, length us, event | category | flops | bytes accessed | tf_op | source)
XLA Modules:
  0.0 262.1 jit_solution(12537288334544157710)
XLA Ops:
  6.5 0.7 all-gather.3.cloned.1.call-update
  7.3 1.2 dynamic_slice.37
  11.2 17.0 %copy.30 = bf16[2048,3,1024]{0,2,1:T(8,128)(2,1)} copy(bf16[2048,3,1024]{2,0,1:T(8,128)(2,1)} %param.27) | data formatting | bytes 25165824 | tf_op args[5]
  28.2 0.2 select_reduce_fusion.2
  28.5 6.5 %copy.47 = bf16[2048,1024]{0,1:T(8,128)(2,1)} copy(bf16[2048,1024]{1,0:T(8,128)(2,1)} %param.37) | data formatting | bytes 8388608 | tf_op jit(solution)/shard_map/reshape.2
  35.0 0.6 select_reduce_fusion.6
  35.7 0.6 add_compare_fusion
  36.3 0.1 multiply_cosine_fusion
  36.5 13.8 %all-gather.3.cloned.1.call-done = bf16[512,1024]{1,0:T(8,128)(2,1)} async-done(((bf16[32,1024]{1,0:T(8,128)(2,1)}), bf16[512,1024]{1,0:T(8,128)(2,1)}) %all-gather.3.cloned.1.call-update) | async-done | bytes 1048592 | tf_op jit(solution)/shard_map/all_gather | solution.py:106
  50.3 1.5 convolution_convert_fusion.1
  51.8 4.9 %all_gather.22 = bf16[32,2048]{1,0:T(8,128)(2,1)S(1)} all-gather(bf16[32,1024]{1,0:T(8,128)(2,1)S(1)} %convolution_convert_fusion.1), channel_id=1, replica_groups=mesh['seq'=16,'head'=2] {'head'}, dimensions={1}, use_global_device_ids=true | all-gather | bytes 196608 | tf_op jit(solution)/shard_map/all_gather | solution.py:112
  56.8 0.1 convert_reduce_fusion
  56.9 0.2 fusion.26
  57.2 8.5 %fusion.15 = f32[32,3,1024]{2,0,1:T(8,128)S(1)} fusion(bf16[2048,3,1024]{0,2,1:T(8,128)(2,1)} %copy.30, f32[3,1024]{1,0:T(4,128)S(1)} %copy-done.1, bf16[32,2048]{1,0:T(8,128)(2,1)S(1)} %all_gather.22, f32[2048]{0:T(1024)S(1)} %copy-done.5, f32[2048]{0:T(1024)S(1)} %copy-done.6, f32[32]{0:T(128)S(1)} %add_rsqrt_fusion, f32[32]{0:T(128)S(1)} %broadcast_multiply_fusion), kind=kOutput, calls=%fused_computation.22 | convolution fusion | flops 403144704 | bytes 13136128 | tf_op jit(solution)/shard_map/dot_general | solution.py:116
  65.9 0.1 slice.84
  66.0 0.1 slice.85
  66.1 0.2 subtract_convert_fusion.1
  66.2 0.3 multiply_reduce_fusion
  66.6 3.4 %fusion.11 = f32[32,4,1,64]{3,2,1,0:T(1,128)S(1)} fusion(bf16[32,8,4,8,256]{4,3,2,1,0:T(8,128)(2,1)} %bitcast.118, bf16[32,4,256,1]{2,1,0,3:T(4,128)(2,1)S(1)} %bitcast.115), kind=kOutput, calls=%fused_computation.16 | convolution fusion | flops 4194304 | bytes 4292608 | tf_op jit(solution)/shard_map/rhc,rthc->rht/dot_general | solution.py:51
  70.0 0.1 fusion.96
  70.1 0.2 fusion.97
  70.3 0.1 select_reduce_fusion.1
  70.4 58.4 %psum.7 = f32[4,4,256]{2,1,0:T(4,128)S(1)} all-reduce(f32[4,4,256]{2,1,0:T(4,128)S(1)} %select_reduce_fusion.1), channel_id=1, replica_groups=mesh['seq'=16,'head'=2] {'seq'}, use_global_device_ids=true, to_apply=%region_8.9 | all-reduce | flops 4096 | bytes 32768 | tf_op jit(solution)/shard_map/psum | solution.py:137
  128.9 3.0 %fusion.108 = f32[4,1,2048]{2,1,0:T(1,128)S(1)} fusion(bf16[2048,4,256]{0,2,1:T(8,128)(2,1)} %bitcast.112, bf16[4,256,1]{1,0,2:T(4,128)(2,1)S(1)} %bitcast.116), kind=kOutput, calls=%fused_computation.149 | convolution fusion | flops 4194304 | bytes 4229120 | tf_op jit(solution)/shard_map/rhc,rthc->rht/dot_general | solution.py:51
  131.9 0.1 fusion.107
  132.0 0.2 fusion.105
  132.3 0.7 fusion.5
  133.0 17.8 %all_gather.25 = f32[16,4,4,256]{3,2,1,0:T(4,128)S(1)} all-gather(f32[1,4,4,256]{3,2,1,0:T(4,128)S(1)} %broadcast_select_fusion), channel_id=1, replica_groups=mesh['seq'=16,'head'=2] {'seq'}, dimensions={0}, use_global_device_ids=true | all-gather | bytes 278528 | tf_op jit(solution)/shard_map/all_gather | solution.py:16
  150.9 19.3 %all_gather.24 = f32[16,4,4]{2,1,0:T(4,128)S(1)} all-gather(f32[1,4,4]{2,1,0:T(4,128)S(1)} %get-tuple-element.228), channel_id=1, replica_groups=mesh['seq'=16,'head'=2] {'seq'}, dimensions={0}, use_global_device_ids=true | all-gather | bytes 1088 | tf_op jit(solution)/shard_map/all_gather | solution.py:16
  170.2 17.7 %all_gather.23 = f32[16,4,4]{2,1,0:T(4,128)S(1)} all-gather(f32[1,4,4]{2,1,0:T(4,128)S(1)} %get-tuple-element.229), channel_id=1, replica_groups=mesh['seq'=16,'head'=2] {'seq'}, dimensions={0}, use_global_device_ids=true | all-gather | bytes 1088 | tf_op jit(solution)/shard_map/all_gather | solution.py:16
  187.9 2.0 while.19
  188.0 0.1 fusion.154
  188.1 0.1 fusion.154
  188.3 0.1 fusion.154
  188.5 0.1 fusion.154
  188.7 0.1 fusion.154
  189.1 0.1 fusion.154
  189.6 0.1 fusion.154
  189.8 0.1 select_reduce_fusion
  190.1 3.0 %fusion.8 = f32[32,4,1,256]{3,2,1,0:T(1,128)S(1)} fusion(bf16[32,8,4,8,256]{4,3,2,1,0:T(8,128)(2,1)} %bitcast.113, bf16[32,4,64,1]{2,0,1,3:T(8,128)(2,1)S(1)} %get-tuple-element.218), kind=kOutput, calls=%fused_computation.13 | convolution fusion | flops 4194304 | bytes 4341760 | tf_op jit(solution)/shard_map/rht,rthc->rhc/dot_general | solution.py:58
  193.2 0.1 fusion.93
  193.4 0.1 copy-done
  193.5 0.8 fusion.143
  194.4 10.0 %fusion.14 = bf16[32,2048]{1,0:T(8,128)(2,1)} fusion(f32[32,2048]{1,0:T(8,128)S(1)} %fusion.143, bf16[2048,2048]{1,0:T(8,128)(2,1)} %param.33, bf16[2048,2048]{1,0:T(8,128)(2,1)} %param.31, bf16[32,2048]{1,0:T(8,128)(2,1)S(1)} %all_gather.22, f32[2048]{0:T(1024)S(1)} %copy-done.2, f32[2048]{0:T(1024)S(1)} %copy-done.3, f32[2048]{0:T(1024)S(1)} %copy-done.4, ...), kind=kOutput, calls=%fused_computation.21 | convolution fusion | flops 541720576 | bytes 17326336 | tf_op jit(solution)/shard_map/dot_general | solution.py:195
  204.5 8.8 %reduce-scatter.2.cloned.1.call-done = bf16[32,1024]{1,0:T(8,128)(2,1)} async-done(((bf16[32,2048]{1,0:T(8,128)(2,1)}), bf16[32,1024]{1,0:T(8,128)(2,1)}) %reduce-scatter.2.cloned.1.call-update) | async-done | bytes 65552 | tf_op jit(solution)/shard_map/reduce_scatter | solution.py:198
  213.2 1.5 add_convert_fusion
  214.8 38.6 %all-gather.5.cloned.1.call-done = bf16[512,1024]{1,0:T(8,128)(2,1)} async-done(((bf16[32,1024]{1,0:T(8,128)(2,1)}), bf16[512,1024]{1,0:T(8,128)(2,1)}) %all-gather.5.cloned.1.call-update) | async-done | bytes 1048592 | tf_op jit(solution)/shard_map/all_gather | solution.py:206
  253.4 2.2 convolution_convert_fusion
  (78 shorter events, 2.2 us)
Async XLA Ops:
  6.5 43.8 %all-gather.3.cloned.1.call-start = ((), (), s32[]{:S(2)}) async-start(), calls=%async_computation.1 | async-start | bytes 1114112 | tf_op jit(solution)/shard_map/all_gather | solution.py:106
  7.3 206.0 %reduce-scatter.2.cloned.1.call-start = ((), (), s32[]{:S(2)}) async-start(), calls=%async_computation.2 | async-start | bytes 196608 | tf_op jit(solution)/shard_map/reduce_scatter | solution.py:198
  11.2 17.0 %copy-start.9 = (s32[512]{0:T(512)S(1)}, s32[512]{0:T(512)}, u32[]{:S(2)}) copy-start(s32[512]{0:T(512)} %param.40) | copy-start | bytes 6148
  11.2 17.1 %copy-start.10 = (s32[512]{0:T(512)S(1)}, s32[512]{0:T(512)}, u32[]{:S(2)}) copy-start(s32[512]{0:T(512)} %param.39) | copy-start | bytes 6148
  28.4 28.7 %copy-start.1 = (f32[3,1024]{1,0:T(4,128)S(1)}, f32[3,1024]{1,0:T(4,128)}, u32[]{:S(2)}) copy-start(f32[3,1024]{1,0:T(4,128)} %param.28) | copy-start | bytes 36868
  28.4 28.7 %copy-start.5 = (f32[2048]{0:T(1024)S(1)}, f32[2048]{0:T(1024)}, u32[]{:S(2)}) copy-start(f32[2048]{0:T(1024)} %param.24) | copy-start | bytes 24580
  28.5 28.7 %copy-start.6 = (f32[2048]{0:T(1024)S(1)}, f32[2048]{0:T(1024)}, u32[]{:S(2)}) copy-start(f32[2048]{0:T(1024)} %param.23) | copy-start | bytes 24580
  128.8 3.4 %copy-start.11 = (bf16[2048,1024]{1,0:T(8,128)(2,1)S(1)}, bf16[2048,1024]{1,0:T(8,128)(2,1)}, u32[]{:S(2)}) copy-start(bf16[2048,1024]{1,0:T(8,128)(2,1)} %param.38) | copy-start | bytes 12582916
  190.1 3.5 %copy-start = (bf16[1024,2048]{1,0:T(8,128)(2,1)S(1)}, bf16[1024,2048]{1,0:T(8,128)(2,1)}, u32[]{:S(2)}) copy-start(bf16[1024,2048]{1,0:T(8,128)(2,1)} %param.29) | copy-start | bytes 12582916
  190.1 4.3 %copy-start.2 = (f32[2048]{0:T(1024)S(1)}, f32[2048]{0:T(1024)}, u32[]{:S(2)}) copy-start(f32[2048]{0:T(1024)} %param.32) | copy-start | bytes 24580
  190.1 4.3 %copy-start.3 = (f32[2048]{0:T(1024)S(1)}, f32[2048]{0:T(1024)}, u32[]{:S(2)}) copy-start(f32[2048]{0:T(1024)} %param.26) | copy-start | bytes 24580
  190.1 4.3 %copy-start.4 = (f32[2048]{0:T(1024)S(1)}, f32[2048]{0:T(1024)}, u32[]{:S(2)}) copy-start(f32[2048]{0:T(1024)} %param.25) | copy-start | bytes 24580
  194.4 18.9 %copy-start.7 = (f32[1024]{0:T(1024)S(1)}, f32[1024]{0:T(1024)}, u32[]{:S(2)}) copy-start(f32[1024]{0:T(1024)} %param.34) | copy-start | bytes 12292
  194.4 18.8 %copy-start.8 = (f32[1024]{0:T(1024)S(1)}, f32[1024]{0:T(1024)}, u32[]{:S(2)}) copy-start(f32[1024]{0:T(1024)} %param.30) | copy-start | bytes 12292
  204.4 49.0 %all-gather.5.cloned.1.call-start = ((), (), s32[]{:S(2)}) async-start(), calls=%async_computation.3 | async-start | bytes 1114112 | tf_op jit(solution)/shard_map/all_gather | solution.py:206
Sparse Core Ops, SparseCore 0:
  9.5 40.7 all-gather.2
  204.5 8.6 reduce-scatter.1
  215.4 37.9 all-gather.4
where the time goes:
time: 263 us; the launch traced here: 262 us
  blocking collectives  118 us (45%)
  waiting for transfers between devices  61.9 us (24%)
  matrix products  33 us (13%)
  local copies, waits for them, and re-layouts  25.6 us (10%)
  between operations  16 us (6%)
  other arithmetic  7.06 us (3%)
    psum x1, blocking collectives, local(): long_queries = lax.psum(long_part, 'seq')  58.4 us
    all_gather x3, blocking collectives, merged(): everything = jax.tree.map(lambda part: lax.all_gather(part, axis), array)  54.8 us
    all_gather x1, waiting for transfers between devices, local(): lax.all_gather(finished, 'seq', axis=0, tiled=True)  38.6 us
    unnamed x25, local copies, waits for them, and re-layouts  17.2 us
    all_gather x1, waiting for transfers between devices, local(): shard_rows = lax.all_gather(tokens, 'seq', axis=0, tiled=True)  13.8 us
    dot_general x1, matrix products, local(): jnp.dot(hidden_units, w_down, preferred_element_type=jnp.float32)  9.99 us
    reduce_scatter x1, waiting for transfers between devices, local(): lax.psum_scatter(partial_sum.astype(jnp.bfloat16), 'head', scatter_dimens...  8.76 us
    dot_general x1, matrix products, local(): jnp.dot(normed_attn, w_qkv.reshape(w_qkv.shape[0], 3 * part_width), prefe...  8.47 us
  transfers between devices with their start and end apart: 3, of which 3 were waited for; matrix products, arithmetic and copies ran while one was open for 10% of the time, Pallas kernels for 0%

commit v1 on v0

v1 whole, which is shorter than its diff:
```python
import functools

import jax
import jax.numpy as jnp
from jax import lax
from jax.experimental import pallas as pl
from jax.experimental.pallas import tpu as pltpu
from jax.sharding import PartitionSpec as P

HD = 256
ROT = 64
LONGS = 4
CAP = 4
MESH = pl.DeviceIdType.MESH

epsilon = 1e-05
very_low = -1e30


def layer_norm(values, gain, shift):
    center = jnp.mean(values, axis=-1, keepdims=True)
    offset = values - center
    spread = jnp.mean(offset * offset, axis=-1, keepdims=True)
    return offset * lax.rsqrt(spread + epsilon) * gain + shift


def rotary(values, position):
    half_rot = ROT // 2
    frequency = jnp.power(10000.0, -2.0 * jnp.arange(half_rot, dtype=jnp.float32) / ROT)
    angles = position.astype(jnp.float32)[:, None] * frequency[None, :]
    cosine = jnp.cos(angles)[:, None, :]
    sine_of = jnp.sin(angles)[:, None, :]
    leading = values[..., :half_rot]
    trailing = values[..., half_rot:ROT]
    return jnp.concatenate(
        [
            leading * cosine - trailing * sine_of,
            trailing * cosine + leading * sine_of,
            values[..., ROT:],
        ],
        axis=-1,
    )


def attend(queries, key_rows, value_rows, usable):
    scores = jnp.einsum(
        "rhc,rthc->rht", queries, key_rows, preferred_element_type=jnp.float32
    ) * HD ** (-0.5)
    masked = jnp.where(usable[:, None, :], scores, very_low)
    summit = jnp.max(masked, axis=-1)
    weights = jnp.where(usable[:, None, :], jnp.exp(masked - summit[..., None]), 0.0)
    amount = jnp.sum(weights, axis=-1)
    mixed = jnp.einsum(
        "rht,rthc->rhc",
        weights.astype(jnp.bfloat16),
        value_rows,
        preferred_element_type=jnp.float32,
    )
    return (summit, amount, mixed)


def device_of(flat, seqs):
    return (lax.rem(flat, seqs), lax.div(flat, seqs))


def greet(me, total, seqs):
    barrier = pltpu.get_barrier_semaphore()

    def hello(k, carry):
        other = lax.rem(me + k, total)
        pl.semaphore_signal(
            barrier, inc=1, device_id=device_of(other, seqs), device_id_type=MESH
        )
        return carry

    lax.fori_loop(1, total, hello, 0)
    pl.semaphore_wait(barrier, total - 1)


def dispatch_kernel(seqs, heads, rows_ref, long_ref, recv_ref, lrecv_ref, ssem, rsem, lssem, lrsem):
    total = seqs * heads
    seq = lax.axis_index("seq")
    head = lax.axis_index("head")
    me = head * seqs + seq
    greet(me, total, seqs)

    def rows_copy(target, source):
        return pltpu.make_async_remote_copy(
            src_ref=rows_ref.at[lax.rem(target, seqs)],
            dst_ref=recv_ref.at[source],
            send_sem=ssem.at[target],
            recv_sem=rsem.at[source],
            device_id=device_of(target, seqs),
            device_id_type=MESH,
        )

    def long_copy(target, source_head):
        return pltpu.make_async_remote_copy(
            src_ref=long_ref,
            dst_ref=lrecv_ref.at[source_head],
            send_sem=lssem.at[target],
            recv_sem=lrsem.at[source_head],
            device_id=device_of(target, seqs),
            device_id_type=MESH,
        )

    def send(k, carry):
        rows_copy(lax.rem(me + k, total), me).start()
        return carry

    def send_long(k, carry):
        long_copy(lax.rem(me + k, total), head).start()
        return carry

    @pl.when(seq == 0)
    def _():
        lax.fori_loop(1, total, send_long, 0)

    lax.fori_loop(1, total, send, 0)
    recv_ref[me] = rows_ref[seq]

    @pl.when(seq == 0)
    def _():
        lrecv_ref[head] = long_ref[...]

    def finish(k, carry):
        rows_copy(lax.rem(me + k, total), me).wait_send()
        rows_copy(me, lax.rem(me + total - k, total)).wait_recv()
        return carry

    lax.fori_loop(1, total, finish, 0)

    def sent_long(k, carry):
        long_copy(lax.rem(me + k, total), head).wait_send()
        return carry

    @pl.when(seq == 0)
    def _():
        lax.fori_loop(1, total, sent_long, 0)

    for source_head in range(heads):

        @pl.when(jnp.logical_or(seq != 0, head != source_head))
        def _():
            long_copy(me, source_head).wait_recv()


def pieces_kernel(seqs, heads, part_ref, recv_ref, ssem, rsem):
    seq = lax.axis_index("seq")
    head = lax.axis_index("head")
    barrier = pltpu.get_barrier_semaphore()

    def hello(k, carry):
        pl.semaphore_signal(
            barrier, inc=1, device_id=(lax.rem(seq + k, seqs), head), device_id_type=MESH
        )
        return carry

    lax.fori_loop(1, seqs, hello, 0)
    pl.semaphore_wait(barrier, seqs - 1)

    def copy(target, source):
        return pltpu.make_async_remote_copy(
            src_ref=part_ref,
            dst_ref=recv_ref.at[source],
            send_sem=ssem.at[target],
            recv_sem=rsem.at[source],
            device_id=(target, head),
            device_id_type=MESH,
        )

    def send(k, carry):
        copy(lax.rem(seq + k, seqs), seq).start()
        return carry

    lax.fori_loop(1, seqs, send, 0)
    recv_ref[seq] = part_ref[...]

    def finish(k, carry):
        copy(lax.rem(seq + k, seqs), seq).wait_send()
        copy(seq, lax.rem(seq + seqs - k, seqs)).wait_recv()
        return carry

    lax.fori_loop(1, seqs, finish, 0)


def return_kernel(seqs, heads, rows_ref, recv_ref, ssem, rsem):
    total = seqs * heads
    seq = lax.axis_index("seq")
    head = lax.axis_index("head")
    me = head * seqs + seq
    greet(me, total, seqs)

    def copy(target, source):
        return pltpu.make_async_remote_copy(
            src_ref=rows_ref.at[target],
            dst_ref=recv_ref.at[source],
            send_sem=ssem.at[target],
            recv_sem=rsem.at[source],
            device_id=device_of(target, seqs),
            device_id_type=MESH,
        )

    def send(k, carry):
        copy(lax.rem(me + k, total), me).start()
        return carry

    lax.fori_loop(1, total, send, 0)
    recv_ref[me] = rows_ref[me]

    def finish(k, carry):
        copy(lax.rem(me + k, total), me).wait_send()
        copy(me, lax.rem(me + total - k, total)).wait_recv()
        return carry

    lax.fori_loop(1, total, finish, 0)


def comm_call(kernel, name, out_shapes, sem_counts, collective_id, *operands):
    vmem = pl.BlockSpec(memory_space=pltpu.VMEM)
    return pl.pallas_call(
        kernel,
        out_shape=out_shapes,
        in_specs=[vmem] * len(operands),
        out_specs=jax.tree.map(lambda _: vmem, out_shapes),
        scratch_shapes=[pltpu.SemaphoreType.DMA((count,)) for count in sem_counts],
        compiler_params=pltpu.CompilerParams(
            collective_id=collective_id, has_side_effects=True
        ),
        name=name,
    )(*operands)


def local(
    seqs,
    heads,
    tokens,
    ln1_gain,
    ln1_shift,
    ln2_gain,
    ln2_shift,
    w_qkv,
    b_qkv,
    w_dense,
    b_dense,
    w_up,
    b_up,
    w_down,
    b_down,
    keys_short,
    values_short,
    keys_long,
    values_long,
    lengths,
    slot_request,
    piece_map,
):
    total = seqs * heads
    slot_rows, part_width = tokens.shape
    width = part_width * heads
    seq_place = lax.axis_index("seq")
    heads_here = part_width // HD
    slots = jnp.arange(slot_request.shape[0], dtype=jnp.int32)
    local_ids = jnp.arange(slot_rows, dtype=jnp.int32)
    cells = jnp.arange(seqs * CAP, dtype=jnp.int32)

    home_ids = seq_place * slot_rows + local_ids
    my_owner = (
        jnp.sum(jnp.where(slot_request[None, :] == home_ids[:, None], slots[None, :], 0), axis=1)
        // slot_rows
    )
    home_rank = jnp.sum(
        (my_owner[None, :] == my_owner[:, None]) & (local_ids[None, :] < local_ids[:, None]),
        axis=1,
        dtype=jnp.int32,
    )
    home_cell = my_owner * CAP + home_rank
    home_select = (cells[:, None] == home_cell[None, :]).astype(jnp.bfloat16)
    home_back = (home_cell[:, None] == cells[None, :]).astype(jnp.bfloat16)
    my_requests = lax.dynamic_slice_in_dim(slot_request, seq_place * slot_rows, slot_rows)
    my_home = my_requests // slot_rows
    slot_rank = jnp.sum(
        (my_home[None, :] == my_home[:, None]) & (my_requests[None, :] < my_requests[:, None]),
        axis=1,
        dtype=jnp.int32,
    )
    slot_cell = my_home * CAP + slot_rank
    slot_select = (slot_cell[:, None] == cells[None, :]).astype(jnp.bfloat16)
    slot_back = (cells[:, None] == slot_cell[None, :]).astype(jnp.bfloat16)

    packed = (
        jnp.dot(home_select, tokens, preferred_element_type=jnp.float32)
        .astype(jnp.bfloat16)
        .reshape(seqs, CAP, part_width)
    )
    arrived, long_rows = comm_call(
        functools.partial(dispatch_kernel, seqs, heads),
        "dispatch",
        (
            jax.ShapeDtypeStruct((total, CAP, part_width), jnp.bfloat16),
            jax.ShapeDtypeStruct((heads, LONGS, part_width), jnp.bfloat16),
        ),
        (total, total, total, heads),
        0,
        packed,
        tokens[:LONGS],
    )
    arrived = arrived.reshape(heads, seqs * CAP, part_width)
    resident = jnp.concatenate(
        [
            jnp.concatenate(
                [
                    jnp.dot(slot_select, arrived[h], preferred_element_type=jnp.float32)
                    for h in range(heads)
                ],
                axis=1,
            ),
            jnp.concatenate([long_rows[h] for h in range(heads)], axis=1).astype(jnp.float32),
        ],
        axis=0,
    )
    normed_attn = layer_norm(resident, ln1_gain, ln1_shift).astype(jnp.bfloat16)
    normed_mlp = layer_norm(resident[:slot_rows], ln2_gain, ln2_shift).astype(jnp.bfloat16)
    parts = [
        jnp.dot(normed_attn, w_qkv[:, j], preferred_element_type=jnp.float32) + b_qkv[j][None]
        for j in range(3)
    ]
    my_lengths = jnp.sum(
        jnp.where(my_requests[:, None] == slots[None, :], lengths[None, :], 0), axis=1
    )
    all_lengths = jnp.concatenate([my_lengths, lengths[:LONGS]])
    rows_all = slot_rows + LONGS
    every_query = rotary(parts[0].reshape(rows_all, heads_here, HD), all_lengths).astype(
        jnp.bfloat16
    )
    queries = every_query[:slot_rows]
    long_queries = every_query[slot_rows:]
    new_keys = rotary(
        parts[1][:slot_rows].reshape(slot_rows, heads_here, HD), my_lengths
    ).astype(jnp.bfloat16)
    new_values = parts[2][:slot_rows].reshape(slot_rows, heads_here, HD).astype(jnp.bfloat16)

    piece_count = seqs // LONGS
    my_piece = lax.dynamic_slice_in_dim(piece_map, seq_place, 1)[0]
    long_owner = my_piece // piece_count
    piece_index = my_piece % piece_count
    long_pick = jnp.arange(LONGS, dtype=jnp.int32) == long_owner
    piece_query = jnp.sum(
        jnp.where(long_pick[:, None, None], long_queries.astype(jnp.float32), 0.0), axis=0
    ).astype(jnp.bfloat16)
    long_length = jnp.sum(jnp.where(long_pick, lengths[:LONGS], 0))
    piece_len = keys_long.shape[0]
    positions = piece_index * piece_len + jnp.arange(piece_len, dtype=jnp.int32)
    piece_usable = (positions < long_length)[None, :]
    piece_top, piece_total, piece_out = attend(
        piece_query[None],
        keys_long.reshape(1, piece_len, heads_here, HD),
        values_long.reshape(1, piece_len, heads_here, HD),
        piece_usable,
    )
    stats = jnp.concatenate(
        [
            jnp.broadcast_to(piece_top[0][:, None], (heads_here, 128)),
            jnp.broadcast_to(piece_total[0][:, None], (heads_here, 128)),
        ],
        axis=1,
    )
    every_piece = comm_call(
        functools.partial(pieces_kernel, seqs, heads),
        "pieces",
        jax.ShapeDtypeStruct((seqs, 2 * heads_here, HD), jnp.float32),
        (seqs, seqs),
        1,
        jnp.concatenate([piece_out[0], stats], axis=0),
    )

    short_max = keys_short.shape[1]
    short_usable = (jnp.arange(short_max, dtype=jnp.int32)[None, :] < my_lengths[:, None]) & (
        my_lengths <= short_max
    )[:, None]
    short_top, short_total, short_out = attend(
        queries,
        keys_short.reshape(slot_rows, short_max, heads_here, HD),
        values_short.reshape(slot_rows, short_max, heads_here, HD),
        short_usable,
    )
    own_score = jnp.sum(
        queries.astype(jnp.float32) * new_keys.astype(jnp.float32), axis=-1
    ) * HD ** (-0.5)

    out_of = every_piece[:, :heads_here]
    top_of = every_piece[:, heads_here:, 0]
    total_of = every_piece[:, heads_here:, 128]
    matches = my_requests[:, None] == (piece_map // piece_count)[None, :]
    spread = jnp.where(matches[:, :, None], top_of[None], very_low)
    summit = jnp.maximum(jnp.maximum(short_top, own_score), jnp.max(spread, axis=1))
    piece_scale = jnp.where(matches[:, :, None], jnp.exp(spread - summit[:, None]), 0.0)
    short_scale = jnp.exp(short_top - summit)
    own_scale = jnp.exp(own_score - summit)
    denominator = (
        short_total * short_scale + own_scale + jnp.sum(piece_scale * total_of[None], axis=1)
    )
    numerator = (
        short_out * short_scale[..., None]
        + new_values.astype(jnp.float32) * own_scale[..., None]
        + jnp.sum(piece_scale[..., None] * out_of[None], axis=1)
    )
    attended = (
        (numerator / denominator[..., None]).reshape(slot_rows, part_width).astype(jnp.bfloat16)
    )
    hidden_units = jax.nn.gelu(
        jnp.dot(normed_mlp, w_up, preferred_element_type=jnp.float32) + b_up, approximate=False
    ).astype(jnp.bfloat16)
    partial_sum = (
        jnp.dot(attended, w_dense, preferred_element_type=jnp.float32)
        + jnp.dot(hidden_units, w_down, preferred_element_type=jnp.float32)
    ).astype(jnp.bfloat16)
    outgoing = jnp.stack(
        [
            jnp.dot(
                slot_back,
                partial_sum[:, h * part_width : (h + 1) * part_width],
                preferred_element_type=jnp.float32,
            ).astype(jnp.bfloat16)
            for h in range(heads)
        ]
    ).reshape(total, CAP, part_width)
    returned = comm_call(
        functools.partial(return_kernel, seqs, heads),
        "give_back",
        jax.ShapeDtypeStruct((total, CAP, part_width), jnp.bfloat16),
        (total, total),
        2,
        outgoing,
    ).reshape(heads, seqs * CAP, part_width)
    head_total = sum(
        jnp.dot(home_back, returned[h], preferred_element_type=jnp.float32) for h in range(heads)
    )
    return (tokens.astype(jnp.float32) + head_total + b_dense + b_down).astype(jnp.bfloat16)


def solution(mesh):
    in_specs = (
        P("seq", "head"),
        P(),
        P(),
        P(),
        P(),
        P(None, None, "head"),
        P(None, "head"),
        P("head", None),
        P("head"),
        P(None, "head"),
        P("head"),
        P("head", None),
        P("head"),
        P("seq", None, "head"),
        P("seq", None, "head"),
        P("seq", "head"),
        P("seq", "head"),
        P(),
        P(),
        P(),
    )
    out_specs = P("seq", "head")
    body = functools.partial(local, mesh.shape["seq"], mesh.shape["head"])
    return jax.shard_map(body, mesh=mesh, in_specs=in_specs, out_specs=out_specs, check_vma=False)
```

time: 263 us -> 105 us (0.40)
  blocking collectives: 118 us -> 0 us
  waiting for transfers between devices: 61.9 us -> 0 us
  Pallas kernels: 0 us -> 40.1 us
  between operations: 16 us -> 3.1 us
  local copies, waits for them, and re-layouts: 25.6 us -> 16.1 us
  matrix products: 33 us -> 36.5 us
    all_gather x4 -> x0, blocking collectives: 59.7 us -> none  [the longest x3 54.8 us: merged(): everything = jax.tree.map(lambda part: lax.all_gather(part, axis), array)]
    psum x1 -> x0, blocking collectives: 58.4 us -> none  [local(): long_queries = lax.psum(long_part, 'seq')]
    all_gather x2 -> x0, waiting for transfers between devices: 52.4 us -> none  [the longest x1 38.6 us: local(): lax.all_gather(finished, 'seq', axis=0, tiled=True)]
    pallas_call x0 -> x3, Pallas kernels: none -> 40.1 us  [comm_call(): pl.pallas_call(kernel, out_shape=out_shapes, in_specs=[vmem] * len(operan...]
    unnamed x25 -> x21, local copies, waits for them, and re-layouts: 17.2 us -> 0.08 us
    reduce_scatter x1 -> x0, waiting for transfers between devices: 8.76 us -> none  [local(): lax.psum_scatter(partial_sum.astype(jnp.bfloat16), 'head', scatter_dimens...]
    slice x1 -> x11, local copies, waits for them, and re-layouts: 0.03 us -> 5.43 us  [the longest x1 1.32 us: local(): tokens[:LONGS]]
    dot_general x3 -> x10, matrix products: 12.2 us -> 12.2 us  [the longest x3 9.23 us: local(): jnp.dot(normed_attn, w_qkv[:, j], preferred_element_type=jnp.float32)]
  transfers between devices with their start and end apart: 3 -> 0, of which waited for: 3 -> 0; matrix products, arithmetic and copies ran while one was open for 10% -> 0% of each run, Pallas kernels for 0% -> 0%
where the time goes in v1:
time: 105 us; the launch traced here: 104 us
  Pallas kernels  40.1 us (38%)
  matrix products  36.5 us (35%)
  local copies, waits for them, and re-layouts  16.1 us (15%)
  other arithmetic  7.63 us (7%)
  between operations  3.1 us (3%)
    pallas_call x3, Pallas kernels, comm_call(): pl.pallas_call(kernel, out_shape=out_shapes, in_specs=[vmem] * len(operan...  40.1 us
    dot_general x1, matrix products, local(): jnp.dot(hidden_units, w_down, preferred_element_type=jnp.float32)  9.37 us
    dot_general x3, matrix products, local(): jnp.dot(normed_attn, w_qkv[:, j], preferred_element_type=jnp.float32)  9.23 us
    another operation x1, local copies, waits for them, and re-layouts  6.69 us
    dot_general x2, matrix products, attend(): jnp.einsum('rhc,rthc->rht', queries, key_rows, preferred_element_type=jnp...  6.2 us
    dot_general x2, matrix products, attend(): jnp.einsum('rht,rthc->rhc', weights.astype(jnp.bfloat16), value_rows, pre...  5.72 us
    dot_general x1, matrix products, local(): jnp.dot(attended, w_dense, preferred_element_type=jnp.float32)  3.01 us

profile of v1, /device:TPU:0, one launch (start us, length us, event | category | flops | bytes accessed | tf_op | source)
XLA Modules:
  0.0 103.5 jit_solution(3292593242909848393)
XLA Ops:
  0.0 0.8 and_select_fusion.1
  0.8 0.2 convert_reduce_fusion
  1.0 0.9 select_reduce_fusion.1
  1.8 0.2 convert_reduce_fusion.1
  2.0 1.0 convolution_convert_fusion.2
  3.1 0.7 reshape.393.rows_ref
  3.8 1.3 %slice.95.long_ref = bf16[4,1024]{1,0:T(4,128)(2,1)} slice(bf16[32,1024]{1,0:T(8,128)(2,1)} %param.20), slice={[0:4], [0:1024]} | slice | bytes 16384 | tf_op jit(solution)/shard_map/slice | solution.py:306
  5.1 16.5 %dispatch.1 = (bf16[32,4,1024]{2,1,0:T(4,128)(2,1)}, bf16[2,4,1024]{2,1,0:T(4,128)(2,1)}) custom-call(bf16[16,4,1024]{2,1,0:T(4,128)(2,1)} %reshape.393.rows_ref, bf16[4,1024]{1,0:T(4,128)(2,1)} %slice.95.long_ref), custom_call_target="tpu_custom_call" | custom-call | tf_op jit(solution)/shard_map/dispatch/pallas_call | solution.py:221
  21.6 1.1 %fusion.148 = (bf16[16,4,1024]{2,1,0:T(4,128)(2,1)S(1)}, bf16[16,4,1024]{2,1,0:T(4,128)(2,1)S(1)}) fusion(bf16[32,4,1024]{2,1,0:T(4,128)(2,1)} %get-tuple-element.7), kind=kLoop, calls=%fused_computation.235 | loop fusion | bytes 524288 | tf_op jit(solution)/shard_map/slice | solution.py:313
  22.7 0.3 fusion.151
  23.1 0.3 fusion.152
  23.4 0.7 slice_bitcast_fusion.2
  24.3 0.2 multiply_reduce_fusion.1
  24.5 0.9 fusion.150
  25.4 3.1 %fusion.19 = f32[36,1024]{1,0:T(8,128)S(1)} fusion(bf16[2048,3,1024]{2,0,1:T(8,128)(2,1)} %param.25, f32[1024]{0:T(1024)S(1)} %bitcast.105, f32[4,2048]{1,0:T(4,128)S(1)} %maximum_convert_fusion, f32[32,1024]{1,0:T(8,128)S(1)} %get-tuple-element.44, f32[32,1024]{1,0:T(8,128)S(1)} %get-tuple-element.42, f32[2048]{0:T(1024)} %param.22, f32[2048]{0:T(1024)} %param.21, ...), kind=kOutput, calls=%fused_computation.25 | convolution fusion | flops 151547904 | bytes 4657440 | tf_op jit(solution)/shard_map/dot_general | solution.py:325
  28.6 0.6 dynamic_slice.7
  31.8 0.6 select_reduce_fusion.4
  32.4 0.2 select_reduce_fusion
  32.7 0.2 multiply_cosine_fusion
  33.1 0.2 pad_maximum_fusion.2
  33.3 3.4 %fusion.6 = f32[32,4,1,64]{3,2,1,0:T(1,128)S(1)} fusion(bf16[32,8,4,8,256]{4,3,2,1,0:T(8,128)(2,1)} %bitcast.106, bf16[32,4,256,1]{2,1,0,3:T(4,128)(2,1)S(1)} %slice_bitcast_fusion), kind=kOutput, calls=%fused_computation.6 | convolution fusion | flops 4194304 | bytes 4292608 | tf_op jit(solution)/shard_map/rhc,rthc->rht/dot_general | solution.py:46
  36.9 0.2 fusion.89
  37.1 3.1 %fusion.11 = f32[36,1024]{1,0:T(8,128)S(1)} fusion(bf16[2048,3,1024]{2,0,1:T(8,128)(2,1)} %param.25, f32[4,2048]{1,0:T(4,128)S(1)} %maximum_convert_fusion, f32[32,1024]{1,0:T(8,128)S(1)} %get-tuple-element.44, f32[32,1024]{1,0:T(8,128)S(1)} %get-tuple-element.42, f32[2048]{0:T(1024)S(1)} %copy-done.7, f32[2048]{0:T(1024)S(1)} %copy-done.8, ...), kind=kOutput, calls=%fused_computation.11 | convolution fusion | flops 151511040 | bytes 4653344 | tf_op jit(solution)/shard_map/dot_general | solution.py:325
  40.2 0.1 multiply_cosine_fusion.1
  40.6 0.2 multiply_reduce_fusion.3
  41.0 6.7 %copy.52 = bf16[2048,1024]{0,1:T(8,128)(2,1)} copy(bf16[2048,1024]{1,0:T(8,128)(2,1)} %param.35) | data formatting | bytes 8388608 | tf_op jit(solution)/shard_map/reshape.7
  47.7 2.8 %fusion.113 = f32[4,1,2048]{2,1,0:T(1,128)S(1)} fusion(bf16[2048,4,256]{0,2,1:T(8,128)(2,1)} %bitcast.94, bf16[4,256,1]{1,0,2:T(4,128)(2,1)S(1)} %bitcast.98), kind=kOutput, calls=%fused_computation.171 | convolution fusion | flops 4194304 | bytes 4229120 | tf_op jit(solution)/shard_map/rhc,rthc->rht/dot_general | solution.py:46
  50.5 0.7 add_compare_fusion
  51.2 0.1 fusion.108
  51.3 0.2 fusion.99
  51.6 2.8 %fusion = f32[4,1,256]{2,1,0:T(1,128)S(1)} fusion(bf16[256,4,8,256]{3,2,1,0:T(8,128)(2,1)} %bitcast.107, bf16[4,2048,1]{1,0,2:T(4,128)(2,1)S(1)} %get-tuple-element.26), kind=kOutput, calls=%fused_computation | convolution fusion | flops 4194304 | bytes 4214784 | tf_op jit(solution)/shard_map/rht,rthc->rhc/dot_general | solution.py:53
  54.5 0.6 maximum_maximum_fusion.part_ref
  55.2 9.5 %pieces.1 = f32[16,8,256]{2,1,0:T(8,128)} custom-call(f32[8,256]{1,0:T(8,128)} %maximum_maximum_fusion.part_ref), custom_call_target="tpu_custom_call" | custom-call | tf_op jit(solution)/shard_map/pieces/pallas_call | solution.py:221
  64.7 0.9 fusion.149
  66.3 2.9 %fusion.3 = f32[32,4,1,256]{3,2,1,0:T(1,128)S(1)} fusion(bf16[32,8,4,8,256]{4,3,2,1,0:T(8,128)(2,1)} %bitcast.95, bf16[32,4,64,1]{2,0,1,3:T(8,128)(2,1)S(1)} %get-tuple-element.25), kind=kOutput, calls=%fused_computation.3 | convolution fusion | flops 4194304 | bytes 4341760 | tf_op jit(solution)/shard_map/rht,rthc->rhc/dot_general | solution.py:53
  69.2 3.1 %fusion.9 = f32[36,1024]{1,0:T(8,128)S(1)} fusion(bf16[2048,3,1024]{2,0,1:T(8,128)(2,1)} %param.25, f32[4,2048]{1,0:T(4,128)S(1)} %maximum_convert_fusion, f32[32,1024]{1,0:T(8,128)S(1)} %get-tuple-element.44, f32[32,1024]{1,0:T(8,128)S(1)} %get-tuple-element.42, f32[2048]{0:T(1024)S(1)} %copy-done.7, f32[2048]{0:T(1024)S(1)} %copy-done.8, ...), kind=kOutput, calls=%fused_computation.9 | convolution fusion | flops 151511040 | bytes 4653344 | tf_op jit(solution)/shard_map/dot_general | solution.py:325
  72.5 0.6 multiply_reduce_fusion
  73.1 0.2 fusion.83
  73.3 3.0 %fusion.153 = f32[32,2048]{1,0:T(8,128)S(1)} fusion(bf16[32,1024]{1,0:T(8,128)(2,1)S(1)} %bitcast.96, bf16[1024,2048]{1,0:T(8,128)(2,1)} %param.27), kind=kOutput, calls=%fused_computation.240 | convolution fusion | flops 134217728 | bytes 4521984 | tf_op jit(solution)/shard_map/dot_general | solution.py:415
  76.3 0.2 multiply_reduce_fusion.2
  76.6 9.4 %fusion.18 = bf16[32,2048]{1,0:T(8,128)(2,1)S(1)} fusion(f32[32,2048]{1,0:T(8,128)S(1)} %fusion.153, bf16[2048,2048]{1,0:T(8,128)(2,1)} %param.31, bf16[2048,2048]{1,0:T(8,128)(2,1)} %param.29, f32[32,1024]{1,0:T(8,128)S(1)} %get-tuple-element.44, f32[32,1024]{1,0:T(8,128)S(1)} %get-tuple-element.42, f32[2048]{0:T(1024)S(1)} %copy-done.1, ...), kind=kOutput, calls=%fused_computation.20 | convolution fusion | flops 541720576 | bytes 17457408 | tf_op jit(solution)/shard_map/dot_general | solution.py:416
  86.0 0.2 fusion.25
  86.2 0.2 fusion.26
  86.4 0.8 reshape.400.rows_ref
  87.2 14.1 %give_back.1 = bf16[32,4,1024]{2,1,0:T(4,128)(2,1)} custom-call(bf16[32,4,1024]{2,1,0:T(4,128)(2,1)} %reshape.400.rows_ref), custom_call_target="tpu_custom_call" | custom-call | tf_op jit(solution)/shard_map/give_back/pallas_call | solution.py:221
  101.3 1.1 %fusion.147 = (bf16[16,4,1024]{2,1,0:T(4,128)(2,1)S(1)}, bf16[16,4,1024]{2,1,0:T(4,128)(2,1)S(1)}) fusion(bf16[32,4,1024]{2,1,0:T(4,128)(2,1)} %give_back.1), kind=kLoop, calls=%fused_computation.234 | loop fusion | bytes 524288 | tf_op jit(solution)/shard_map/slice | solution.py:437
  102.4 0.2 fusion.105
  102.7 0.9 fusion.27
  (73 shorter events, 2.6 us)
Async XLA Ops:
  3.1 25.5 %copy-start.9 = (s32[16]{0:T(128)S(1)}, s32[16]{0:T(128)}, u32[]{:S(2)}) copy-start(s32[16]{0:T(128)} %param.39) | copy-start | bytes 196
  3.1 28.7 %copy-start.6 = (s32[512]{0:T(512)S(1)}, s32[512]{0:T(512)}, u32[]{:S(2)}) copy-start(s32[512]{0:T(512)} %param.37) | copy-start | bytes 6148
  28.5 8.6 %copy-start.7 = (f32[2048]{0:T(1024)S(1)}, f32[2048]{0:T(1024)}, u32[]{:S(2)}) copy-start(f32[2048]{0:T(1024)} %param.22) | copy-start | bytes 24580
  28.5 8.6 %copy-start.8 = (f32[2048]{0:T(1024)S(1)}, f32[2048]{0:T(1024)}, u32[]{:S(2)}) copy-start(f32[2048]{0:T(1024)} %param.21) | copy-start | bytes 24580
  66.3 6.2 %slice-start = ((f32[16,8,256]{2,1,0:T(8,128)}), f32[16,4,256]{2,1,0:T(4,128)S(1)}, s32[]{:S(2)}) async-start(f32[16,8,256]{2,1,0:T(8,128)} %pieces.1), calls=%async_computation | async-start | bytes 131072 | tf_op jit(solution)/shard_map/slice | solution.py:391
  72.3 4.3 %copy-start.1 = (f32[2048]{0:T(1024)S(1)}, f32[2048]{0:T(1024)}, u32[]{:S(2)}) copy-start(f32[2048]{0:T(1024)} %param.30) | copy-start | bytes 24580
  72.3 4.3 %copy-start.2 = (f32[2048]{0:T(1024)S(1)}, f32[2048]{0:T(1024)}, u32[]{:S(2)}) copy-start(f32[2048]{0:T(1024)} %param.24) | copy-start | bytes 24580
  72.3 4.3 %copy-start.3 = (f32[2048]{0:T(1024)S(1)}, f32[2048]{0:T(1024)}, u32[]{:S(2)}) copy-start(f32[2048]{0:T(1024)} %param.23) | copy-start | bytes 24580
  76.6 26.1 %copy-start = (bf16[32,1024]{1,0:T(8,128)(2,1)S(1)}, bf16[32,1024]{1,0:T(8,128)(2,1)}, u32[]{:S(2)}) copy-start(bf16[32,1024]{1,0:T(8,128)(2,1)} %param.20) | copy-start | bytes 196612
  76.6 26.1 %copy-start.4 = (f32[1024]{0:T(1024)S(1)}, f32[1024]{0:T(1024)}, u32[]{:S(2)}) copy-start(f32[1024]{0:T(1024)} %param.32) | copy-start | bytes 12292
  76.6 26.1 %copy-start.5 = (f32[1024]{0:T(1024)S(1)}, f32[1024]{0:T(1024)}, u32[]{:S(2)}) copy-start(f32[1024]{0:T(1024)} %param.28) | copy-start | bytes 12292

commit v2 on v0

v2 whole, which is shorter than its diff:
```python
import functools

import jax
import jax.numpy as jnp
import numpy as np
from jax import lax
from jax.experimental import pallas as pl
from jax.experimental.pallas import tpu as pltpu
from jax.sharding import PartitionSpec as P

HD = 256
ROT = 64
LONGS = 4
CAP = 4
BLOCK = 2 * CAP
PAD = 8
STATS = 128
MESH = pl.DeviceIdType.MESH
F32 = jnp.float32
BF16 = jnp.bfloat16

epsilon = 1e-05
very_low = -1e30


def iota(shape, axis):
    return lax.broadcasted_iota(jnp.int32, shape, axis)


def onehot(mask):
    return jnp.where(mask, 1.0, 0.0).astype(BF16)


def turned(mask):
    return jnp.where(mask, 1.0, 0.0).astype(F32).T.astype(BF16)


def dot(a, b, **kw):
    return jnp.dot(a, b, preferred_element_type=F32, **kw)


def dot_t(a, b):
    return lax.dot_general(a, b, (((1,), (1,)), ((), ())), preferred_element_type=F32)


def at_block(ref, index):
    return ref.at[pl.ds(pl.multiple_of(index * BLOCK, BLOCK), BLOCK)]


def total_of(values, axis):
    return jnp.sum(values, axis=axis, keepdims=True)


def layer_norm(values, gain, shift):
    center = jnp.mean(values, axis=-1, keepdims=True)
    offset = values - center
    spread = jnp.mean(offset * offset, axis=-1, keepdims=True)
    return offset * lax.rsqrt(spread + epsilon) * gain + shift


def matmul_into(out_ref, x_ref, w_ref, tile):
    def step(i, carry):
        cols = pl.ds(pl.multiple_of(i * tile, tile), tile)
        out_ref[:, cols] = dot(x_ref[...], w_ref[:, cols])
        return carry

    lax.fori_loop(0, w_ref.shape[1] // tile, step, 0)


def layer_kernel(
    seqs,
    heads,
    tokens_ref,
    ln1_gain,
    ln1_shift,
    ln2_gain,
    ln2_shift,
    b_qkv,
    b_out,
    b_up,
    lengths_ref,
    slots_row_ref,
    slots_ref,
    pieces_ref,
    freq_ref,
    w_qkv_hbm,
    w_dense_hbm,
    w_up_hbm,
    w_down_hbm,
    ks_hbm,
    vs_hbm,
    kl_hbm,
    vl_hbm,
    out_ref,
    w_qkv,
    w_dense,
    w_up,
    w_down,
    ks,
    vs,
    kl,
    vl,
    pack,
    recv,
    long_pack,
    long_recv,
    part,
    part_recv,
    back,
    back_recv,
    x1,
    x2,
    qkv,
    up,
    hidden,
    attended,
    dense,
    down,
    load_sem,
    self_sem,
    ssem,
    rsem,
    lssem,
    lrsem,
    pssem,
    prsem,
    bssem,
    brsem,
):
    total = seqs * heads
    seq = lax.axis_index("seq")
    head = lax.axis_index("head")
    me = head * seqs + seq
    rows, width_here = tokens_ref.shape
    half = width_here // 2
    heads_here = width_here // HD
    cells = seqs * BLOCK
    requests = slots_row_ref.shape[1]
    short_max = ks.shape[0] // rows
    piece_len = kl.shape[0]
    piece_count = seqs // LONGS

    def device_of(flat):
        return (lax.rem(flat, seqs), lax.div(flat, seqs))

    loads = [
        pltpu.make_async_copy(src, dst, load_sem.at[i])
        for i, (src, dst) in enumerate(
            [
                (w_qkv_hbm.at[0], w_qkv.at[0]),
                (kl_hbm, kl),
                (w_qkv_hbm.at[1], w_qkv.at[1]),
                (w_qkv_hbm.at[2], w_qkv.at[2]),
                (vl_hbm, vl),
                (w_up_hbm, w_up),
                (w_down_hbm, w_down),
                (ks_hbm, ks),
                (vs_hbm, vs),
                (w_dense_hbm, w_dense),
            ]
        )
    ]
    load_q, load_kl, load_k, load_v, load_vl, load_up, load_down, load_ks, load_vs, load_d = loads

    barrier = pltpu.get_barrier_semaphore()

    def hello(k, carry):
        pl.semaphore_signal(
            barrier, inc=1, device_id=device_of(lax.rem(me + k, total)), device_id_type=MESH
        )
        return carry

    lax.fori_loop(1, total, hello, 0)
    for load in loads:
        load.start()

    slots_row = slots_row_ref[...]
    row_ids = iota((rows, 1), 0)
    lanes_all = iota((rows, requests), 1)
    home_ids = row_ids + seq * rows
    position = total_of(jnp.where(slots_row == home_ids, lanes_all, 0), 1)
    my_req = total_of(jnp.where(lanes_all == home_ids, slots_row, 0), 1)
    my_len = total_of(jnp.where(lanes_all == my_req, lengths_ref[...], 0), 1)
    req_row = slots_ref[pl.ds(seq, 1), :]
    group = iota((rows, seqs), 1)
    in_owner = (position >= group * rows) & (position < (group + 1) * rows)
    in_home = (my_req >= group * rows) & (my_req < (group + 1) * rows)
    owner_hot = onehot(in_owner)
    home_hot = onehot(in_home)
    col_ids = iota((rows, rows), 1)
    rank_home = total_of(
        jnp.where(col_ids < row_ids, dot_t(owner_hot, owner_hot), 0.0), 1
    ).astype(jnp.int32)
    rank_slot = total_of(
        jnp.where(req_row < my_req, dot_t(home_hot, home_hot), 0.0), 1
    ).astype(jnp.int32)
    home_cell = total_of(jnp.where(in_owner, group, 0), 1) * BLOCK + rank_home
    slot_cell = total_of(jnp.where(in_home, group, 0), 1) * BLOCK + rank_slot
    lanes = iota((rows, cells), 1)
    home_lo, home_hi = lanes == home_cell, lanes == home_cell + CAP
    slot_lo, slot_hi = lanes == slot_cell, lanes == slot_cell + CAP

    tok = tokens_ref[...]
    pack[...] = (dot(turned(home_lo), tok[:, :half]) + dot(turned(home_hi), tok[:, half:])).astype(
        BF16
    )
    place = iota((BLOCK, rows), 0)
    source_row = iota((BLOCK, rows), 1)
    long_pack[...] = (
        dot(onehot((source_row == place) & (place < LONGS)), tok[:, :half])
        + dot(onehot((source_row + LONGS == place) & (place >= LONGS)), tok[:, half:])
    ).astype(BF16)

    pl.semaphore_wait(barrier, total - 1)

    def rows_copy(target, source):
        return pltpu.make_async_remote_copy(
            src_ref=at_block(pack, lax.rem(target, seqs)),
            dst_ref=at_block(recv, source),
            send_sem=ssem.at[target],
            recv_sem=rsem.at[source],
            device_id=device_of(target),
            device_id_type=MESH,
        )

    def long_copy(target, source_head):
        return pltpu.make_async_remote_copy(
            src_ref=long_pack,
            dst_ref=at_block(long_recv, source_head),
            send_sem=lssem.at[target],
            recv_sem=lrsem.at[source_head],
            device_id=device_of(target),
            device_id_type=MESH,
        )

    def send_long(k, carry):
        long_copy(lax.rem(me + k, total), head).start()
        return carry

    @pl.when(seq == 0)
    def _():
        lax.fori_loop(1, total, send_long, 0)
        own_long = pltpu.make_async_copy(long_pack, at_block(long_recv, head), self_sem.at[0])
        own_long.start()
        own_long.wait()

    def send(k, carry):
        rows_copy(lax.rem(me + k, total), me).start()
        return carry

    lax.fori_loop(1, total, send, 0)
    own_rows = pltpu.make_async_copy(at_block(pack, seq), at_block(recv, me), self_sem.at[1])
    own_rows.start()

    request_lanes = iota((1, requests), 1)
    my_piece = total_of(jnp.where(iota((1, seqs), 1) == seq, pieces_ref[...], 0), 1)
    long_owner = jnp.zeros_like(my_piece)
    for k in range(1, LONGS):
        long_owner = long_owner + jnp.where(my_piece >= k * piece_count, 1, 0)
    piece_index = my_piece - long_owner * piece_count
    long_len = total_of(jnp.where(request_lanes == long_owner, lengths_ref[...], 0), 1)
    long_limit = long_len - piece_index * piece_len

    all_len = jnp.concatenate([my_len, jnp.broadcast_to(long_len, (PAD, 1))], axis=0)
    angles = all_len.astype(F32) * freq_ref[...]
    lane128 = iota(angles.shape, 1)
    cosine = jnp.where(lane128 < ROT, jnp.cos(angles), 1.0)
    sine = jnp.sin(angles)
    sine_a = jnp.where(lane128 < ROT // 2, -sine, 0.0)
    sine_b = jnp.where((lane128 >= ROT // 2) & (lane128 < ROT), sine, 0.0)

    def spread_table(table, rest):
        filler = jnp.full((table.shape[0], HD - 128), rest, F32)
        return jnp.concatenate([table, filler] * heads_here, axis=1)

    cosine = spread_table(cosine, 1.0)
    sine_a = spread_table(sine_a, 0.0)
    sine_b = spread_table(sine_b, 0.0)

    def rotary(values, n):
        return (
            values * cosine[:n]
            + pltpu.roll(values, width_here - ROT // 2, 1) * sine_a[:n]
            + pltpu.roll(values, ROT // 2, 1) * sine_b[:n]
        )

    own_rows.wait()

    def arrive(k, carry):
        rows_copy(me, lax.rem(me + total - k, total)).wait_recv()
        return carry

    lax.fori_loop(1, total, arrive, 0)
    for source_head in range(heads):

        @pl.when(jnp.logical_or(seq != 0, head != source_head))
        def _():
            long_copy(me, source_head).wait_recv()

    pick_lo, pick_hi = onehot(slot_lo), onehot(slot_hi)
    row8, col8 = iota((PAD, BLOCK), 0), iota((PAD, BLOCK), 1)
    long_lo = onehot((row8 == 0) & (col8 == long_owner))
    long_hi = onehot((row8 == 0) & (col8 == long_owner + LONGS))
    columns = []
    long_columns = []
    for h in range(heads):
        block = recv[h * cells : (h + 1) * cells, :]
        lblock = long_recv[h * BLOCK : (h + 1) * BLOCK, :]
        columns += [dot(pick_lo, block), dot(pick_hi, block)]
        long_columns += [dot(long_lo, lblock), dot(long_hi, lblock)]
    resident = jnp.concatenate(
        [jnp.concatenate(columns, axis=1), jnp.concatenate(long_columns, axis=1)], axis=0
    )
    x1[...] = layer_norm(resident, ln1_gain[...], ln1_shift[...]).astype(BF16)
    x2[...] = layer_norm(resident[:rows], ln2_gain[...], ln2_shift[...]).astype(BF16)

    scale = HD ** (-0.5)
    load_q.wait()
    matmul_into(qkv.at[0], x1, w_qkv.at[0], TILE)
    query = rotary(qkv[0] + b_qkv[0:1, :], rows + PAD)
    lane_here = iota((PAD, width_here), 1)
    head_row = iota((PAD, width_here), 0)
    own_lanes = (lane_here >= head_row * HD) & (lane_here < (head_row + 1) * HD)
    long_query = jnp.where(own_lanes, query[rows : rows + 1], 0.0).astype(BF16)
    query = query[:rows].astype(BF16)
    load_kl.wait()
    scores = dot_t(long_query, kl[...]) * scale
    usable = iota(scores.shape, 1) < long_limit
    masked = jnp.where(usable, scores, very_low)
    piece_top = jnp.max(masked, axis=1, keepdims=True)
    weights = jnp.where(usable, jnp.exp(masked - piece_top), 0.0)
    piece_total = total_of(weights, 1)
    load_vl.wait()
    mixed = dot(weights.astype(BF16), vl[...])
    rowh = iota((PAD, HD), 0)
    piece_out = jnp.zeros((PAD, HD), F32)
    for h in range(heads_here):
        piece_out = jnp.where(rowh == h, mixed[:, h * HD : (h + 1) * HD], piece_out)
    stat_lane = iota((PAD, STATS), 1)
    part[...] = jnp.concatenate(
        [piece_out, jnp.where(stat_lane < STATS // 2, piece_top, piece_total)], axis=1
    )

    def part_copy(target, source):
        return pltpu.make_async_remote_copy(
            src_ref=part,
            dst_ref=at_block(part_recv, source),
            send_sem=pssem.at[target],
            recv_sem=prsem.at[source],
            device_id=(target, head),
            device_id_type=MESH,
        )

    def send_part(k, carry):
        part_copy(lax.rem(seq + k, seqs), seq).start()
        return carry

    lax.fori_loop(1, seqs, send_part, 0)
    own_part = pltpu.make_async_copy(part, at_block(part_recv, seq), self_sem.at[2])
    own_part.start()

    load_k.wait()
    matmul_into(qkv.at[1], x1, w_qkv.at[1], TILE)
    load_v.wait()
    matmul_into(qkv.at[2], x1, w_qkv.at[2], TILE)
    new_key = rotary(qkv[1][:rows] + b_qkv[1:2, :], rows).astype(BF16)
    new_value = (qkv[2][:rows] + b_qkv[2:3, :]).astype(BF16).astype(F32)
    product = query.astype(F32) * new_key.astype(F32)

    load_up.wait()
    matmul_into(up, x2, w_up, TILE)
    before = up[...] + b_up[...]
    hidden[...] = (0.5 * before * (1.0 + lax.erf(before * (0.5**0.5)))).astype(BF16)
    load_down.wait()
    matmul_into(down, hidden, w_down, TILE)

    lane_q = iota((rows, width_here), 1)
    query32 = query.astype(F32)
    split = jnp.concatenate(
        [
            jnp.where((lane_q >= h * HD) & (lane_q < (h + 1) * HD), query32, 0.0)
            for h in range(heads_here)
        ],
        axis=0,
    ).astype(BF16)
    load_ks.wait()
    scores = dot_t(split, ks[...]) * scale
    first = jnp.concatenate([row_ids * short_max] * heads_here, axis=0)
    count = jnp.where(my_len <= short_max, my_len, 0)
    last = first + jnp.concatenate([count] * heads_here, axis=0)
    column = iota(scores.shape, 1)
    usable = (column >= first) & (column < last)
    masked = jnp.where(usable, scores, very_low)
    short_top = jnp.max(masked, axis=1, keepdims=True)
    weights = jnp.where(usable, jnp.exp(masked - short_top), 0.0)
    short_total = total_of(weights, 1)
    load_vs.wait()
    short_out = dot(weights.astype(BF16), vs[...])

    own_part.wait()

    def part_arrive(k, carry):
        part_copy(seq, lax.rem(seq + seqs - k, seqs)).wait_recv()
        return carry

    lax.fori_loop(1, seqs, part_arrive, 0)
    expand = onehot(
        (iota((seqs, cells), 1) >= BLOCK * iota((seqs, cells), 0))
        & (iota((seqs, cells), 1) < BLOCK * iota((seqs, cells), 0) + BLOCK)
    )
    piece_lane = dot(
        jnp.broadcast_to(pieces_ref[...].astype(F32), (PAD, seqs)).astype(BF16), expand
    )[0:1, :]
    first_lane = my_req.astype(F32) * piece_count
    matches = (piece_lane >= first_lane) & (piece_lane < first_lane + piece_count)
    stats = part_recv[:, HD:].T
    tops, totals = stats[0:1, :], stats[STATS // 2 : STATS // 2 + 1, :]
    place_in = lax.bitwise_and(lanes, BLOCK - 1)
    for h in range(heads_here):
        here = slice(h * HD, (h + 1) * HD)
        band = slice(h * rows, (h + 1) * rows)
        own_score = total_of(product[:, here], 1) * scale
        pick = matches & (place_in == h)
        spread = jnp.where(pick, tops, very_low)
        summit = jnp.maximum(
            jnp.maximum(short_top[band], own_score), jnp.max(spread, axis=1, keepdims=True)
        )
        piece_scale = jnp.where(pick, jnp.exp(spread - summit), 0.0)
        short_scale = jnp.exp(short_top[band] - summit)
        own_scale = jnp.exp(own_score - summit)
        denominator = (
            short_total[band] * short_scale + own_scale + total_of(piece_scale * totals, 1)
        )
        numerator = (
            short_out[band, here] * short_scale
            + new_value[:, here] * own_scale
            + dot(piece_scale, part_recv[:, :HD], precision=lax.Precision.HIGHEST)
        )
        attended[:, here] = (numerator / denominator).astype(BF16)
    load_d.wait()
    matmul_into(dense, attended, w_dense, TILE)

    give_lo, give_hi = turned(slot_lo), turned(slot_hi)
    for h in range(heads):
        cols = slice(h * width_here, h * width_here + half)
        rest = slice(h * width_here + half, (h + 1) * width_here)
        back[h * cells : (h + 1) * cells, :] = (
            dot(give_lo, (dense[:, cols] + down[:, cols]).astype(BF16))
            + dot(give_hi, (dense[:, rest] + down[:, rest]).astype(BF16))
        ).astype(BF16)

    def back_copy(target, source):
        return pltpu.make_async_remote_copy(
            src_ref=at_block(back, target),
            dst_ref=at_block(back_recv, source),
            send_sem=bssem.at[target],
            recv_sem=brsem.at[source],
            device_id=device_of(target),
            device_id_type=MESH,
        )

    def send_back(k, carry):
        back_copy(lax.rem(me + k, total), me).start()
        return carry

    lax.fori_loop(1, total, send_back, 0)
    own_back = pltpu.make_async_copy(at_block(back, me), at_block(back_recv, me), self_sem.at[3])
    own_back.start()

    def sent(k, carry):
        target = lax.rem(me + k, total)
        rows_copy(target, me).wait_send()
        return carry

    lax.fori_loop(1, total, sent, 0)

    def sent_part(k, carry):
        part_copy(lax.rem(seq + k, seqs), seq).wait_send()
        return carry

    lax.fori_loop(1, seqs, sent_part, 0)

    def sent_long(k, carry):
        long_copy(lax.rem(me + k, total), head).wait_send()
        return carry

    @pl.when(seq == 0)
    def _():
        lax.fori_loop(1, total, sent_long, 0)

    own_back.wait()

    def back_arrive(k, carry):
        back_copy(lax.rem(me + k, total), me).wait_send()
        back_copy(me, lax.rem(me + total - k, total)).wait_recv()
        return carry

    lax.fori_loop(1, total, back_arrive, 0)
    take_lo, take_hi = onehot(home_lo), onehot(home_hi)
    low = jnp.zeros((rows, half), F32)
    high = jnp.zeros((rows, half), F32)
    for h in range(heads):
        block = back_recv[h * cells : (h + 1) * cells, :]
        low = low + dot(take_lo, block)
        high = high + dot(take_hi, block)
    finished = tokens_ref[...].astype(F32) + jnp.concatenate([low, high], axis=1)
    out_ref[...] = (finished + b_out[0:1, :] + b_out[1:2, :]).astype(BF16)


TILE = 512


def local(
    seqs,
    heads,
    tokens,
    ln1_gain,
    ln1_shift,
    ln2_gain,
    ln2_shift,
    w_qkv,
    b_qkv,
    w_dense,
    b_dense,
    w_up,
    b_up,
    w_down,
    b_down,
    keys_short,
    values_short,
    keys_long,
    values_long,
    lengths,
    slot_request,
    piece_map,
):
    total = seqs * heads
    rows, width_here = tokens.shape
    width = width_here * heads
    units = w_up.shape[1]
    half = width_here // 2
    short_rows = rows * keys_short.shape[1]
    exponent = -2.0 * (np.arange(128) % (ROT // 2)) / ROT
    freq = jnp.asarray(np.power(10000.0, exponent).astype(np.float32)[None])
    vmem = pl.BlockSpec(memory_space=pltpu.VMEM)
    hbm = pl.BlockSpec(memory_space=pl.ANY)
    dma = pltpu.SemaphoreType.DMA
    return pl.pallas_call(
        functools.partial(layer_kernel, seqs, heads),
        out_shape=jax.ShapeDtypeStruct((rows, width_here), BF16),
        in_specs=[vmem] * 13 + [hbm] * 8,
        out_specs=vmem,
        scratch_shapes=[
            pltpu.VMEM((3, width, width_here), BF16),
            pltpu.VMEM((width_here, width), BF16),
            pltpu.VMEM((width, units), BF16),
            pltpu.VMEM((units, width), BF16),
            pltpu.VMEM((short_rows, width_here), BF16),
            pltpu.VMEM((short_rows, width_here), BF16),
            pltpu.VMEM(keys_long.shape, BF16),
            pltpu.VMEM(values_long.shape, BF16),
            pltpu.VMEM((seqs * BLOCK, half), BF16),
            pltpu.VMEM((total * BLOCK, half), BF16),
            pltpu.VMEM((BLOCK, half), BF16),
            pltpu.VMEM((heads * BLOCK, half), BF16),
            pltpu.VMEM((PAD, HD + STATS), F32),
            pltpu.VMEM((seqs * PAD, HD + STATS), F32),
            pltpu.VMEM((total * BLOCK, half), BF16),
            pltpu.VMEM((total * BLOCK, half), BF16),
            pltpu.VMEM((rows + PAD, width), BF16),
            pltpu.VMEM((rows, width), BF16),
            pltpu.VMEM((3, rows + PAD, width_here), F32),
            pltpu.VMEM((rows, units), F32),
            pltpu.VMEM((rows, units), BF16),
            pltpu.VMEM((rows, width_here), BF16),
            pltpu.VMEM((rows, width), F32),
            pltpu.VMEM((rows, width), F32),
            dma((10,)),
            dma((4,)),
            dma((total,)),
            dma((total,)),
            dma((total,)),
            dma((heads,)),
            dma((seqs,)),
            dma((seqs,)),
            dma((total,)),
            dma((total,)),
        ],
        compiler_params=pltpu.CompilerParams(
            collective_id=0, has_side_effects=True, vmem_limit_bytes=66_500_000
        ),
        name="layer",
    )(
        tokens,
        ln1_gain[None],
        ln1_shift[None],
        ln2_gain[None],
        ln2_shift[None],
        b_qkv,
        jnp.stack([b_dense, b_down]),
        b_up[None],
        lengths[None],
        slot_request[None],
        slot_request.reshape(seqs, rows),
        piece_map[None],
        freq,
        jnp.transpose(w_qkv, (1, 0, 2)),
        w_dense,
        w_up,
        w_down,
        keys_short.reshape(short_rows, width_here),
        values_short.reshape(short_rows, width_here),
        keys_long,
        values_long,
    )


def solution(mesh):
    in_specs = (
        P("seq", "head"),
        P(),
        P(),
        P(),
        P(),
        P(None, None, "head"),
        P(None, "head"),
        P("head", None),
        P("head"),
        P(None, "head"),
        P("head"),
        P("head", None),
        P("head"),
        P("seq", None, "head"),
        P("seq", None, "head"),
        P("seq", "head"),
        P("seq", "head"),
        P(),
        P(),
        P(),
    )
    out_specs = P("seq", "head")
    body = functools.partial(local, mesh.shape["seq"], mesh.shape["head"])
    return jax.shard_map(body, mesh=mesh, in_specs=in_specs, out_specs=out_specs, check_vma=False)
```

time: 263 us -> 46 us (0.17)
  blocking collectives: 118 us -> 0 us
  waiting for transfers between devices: 61.9 us -> 0 us
  Pallas kernels: 0 us -> 41.6 us
  matrix products: 33 us -> 0 us
  local copies, waits for them, and re-layouts: 25.6 us -> 2.82 us
  between operations: 16 us -> 0.01 us
  other arithmetic: 7.06 us -> 1.31 us
    all_gather x4 -> x0, blocking collectives: 59.7 us -> none  [the longest x3 54.8 us: merged(): everything = jax.tree.map(lambda part: lax.all_gather(part, axis), array)]
    psum x1 -> x0, blocking collectives: 58.4 us -> none  [local(): long_queries = lax.psum(long_part, 'seq')]
    all_gather x2 -> x0, waiting for transfers between devices: 52.4 us -> none  [the longest x1 38.6 us: local(): lax.all_gather(finished, 'seq', axis=0, tiled=True)]
    pallas_call x0 -> x1, Pallas kernels: none -> 41.6 us  [local(): pl.pallas_call(functools.partial(layer_kernel, seqs, heads), out_shape=ja...]
    dot_general x9 -> x0, matrix products: 33 us -> none  [the longest x1 9.99 us: local(): jnp.dot(hidden_units, w_down, preferred_element_type=jnp.float32)]
    unnamed x25 -> x1, local copies, waits for them, and re-layouts: 17.2 us -> 1.47 us
    reduce_scatter x1 -> x0, waiting for transfers between devices: 8.76 us -> none  [local(): lax.psum_scatter(partial_sum.astype(jnp.bfloat16), 'head', scatter_dimens...]
    another operation x3 -> x0, local copies, waits for them, and re-layouts: 6.66 us -> none
  transfers between devices with their start and end apart: 3 -> 0, of which waited for: 3 -> 0; matrix products, arithmetic and copies ran while one was open for 10% -> 0% of each run, Pallas kernels for 0% -> 0%
where the time goes in v2:
time: 46 us; the launch traced here: 45.7 us
  Pallas kernels  41.6 us (90%)
  local copies, waits for them, and re-layouts  2.82 us (6%)
  other arithmetic  1.31 us (3%)
    pallas_call x1, Pallas kernels, local(): pl.pallas_call(functools.partial(layer_kernel, seqs, heads), out_shape=ja...  41.6 us
    unnamed x1, local copies, waits for them, and re-layouts  1.47 us
    reshape x1, local copies, waits for them, and re-layouts, local(): slot_request.reshape(seqs, rows)  1.35 us
    another operation x1, other arithmetic, local(): jnp.stack([b_dense, b_down])  1.31 us

profile of v2, /device:TPU:0, one launch (start us, length us, event | category | flops | bytes accessed | tf_op | source)
XLA Modules:
  0.0 45.7 jit_solution(16487190567016544029)
XLA Ops:
  0.0 1.3 %pad_maximum_fusion.b_out = f32[2,1024]{1,0:T(2,128)} fusion(f32[1,1024]{1,0:T(1,128)} %bitcast.22, f32[1,1024]{1,0:T(1,128)} %bitcast.23), kind=kLoop, calls=%fused_computation | loop fusion | flops 2048 | bytes 16384 | tf_op jit(solution)/shard_map/stack | solution.py:600
  1.3 1.3 %reshape.9.slots_ref = s32[16,32]{1,0:T(8,128)} reshape(s32[512]{0:T(512)} %param.39) | data formatting | bytes 4096 | tf_op jit(solution)/shard_map/reshape | solution.py:604
  2.7 41.6 %layer.1 = bf16[32,1024]{1,0:T(8,128)(2,1)} custom-call(bf16[32,1024]{1,0:T(8,128)(2,1)} %tokens_ref.1, f32[1,2048]{1,0:T(1,128)} %bitcast.16, f32[1,2048]{1,0:T(1,128)} %bitcast.17, f32[1,2048]{1,0:T(1,128)} %bitcast.18, f32[1,2048]{1,0:T(1,128)} %bitcast.19, f32[3,1024]{1,0:T(4,128)} %b_qkv.1, f32[2,1024]{1,0:T(2,128)} %pad_maximum_fusion.b_out, ...), custom_call_target="tpu_custom_call" | custom-call | tf_op jit(solution)/shard_map/layer/pallas_call | solution.py:548
  44.3 1.5 %copy.23 = bf16[32,1024]{1,0:T(8,128)(2,1)} copy(bf16[32,1024]{1,0:T(8,128)(2,1)} %layer.1) | data formatting | bytes 131072

commit v3 on v2

--- a/solution.py
+++ b/solution.py
@@ -70,19 +70,19 @@
 def layer_kernel(
     seqs,
     heads,
-    tokens_ref,
-    ln1_gain,
-    ln1_shift,
-    ln2_gain,
-    ln2_shift,
-    b_qkv,
-    b_out,
-    b_up,
-    lengths_ref,
-    slots_row_ref,
-    slots_ref,
-    pieces_ref,
-    freq_ref,
+    tokens_hbm,
+    slots_hbm,
+    lengths_hbm,
+    pieces_hbm,
+    freq_hbm,
+    ln1_gain_hbm,
+    ln1_shift_hbm,
+    ln2_gain_hbm,
+    ln2_shift_hbm,
+    b_qkv_hbm,
+    b_dense_hbm,
+    b_down_hbm,
+    b_up_hbm,
     w_qkv_hbm,
     w_dense_hbm,
     w_up_hbm,
@@ -92,6 +92,19 @@
     kl_hbm,
     vl_hbm,
     out_ref,
+    tokens_ref,
+    slots_row_ref,
+    lengths_ref,
+    pieces_ref,
+    freq_ref,
+    ln1_gain,
+    ln1_shift,
+    ln2_gain,
+    ln2_shift,
+    b_qkv,
+    b_dense,
+    b_down,
+    b_up,
     w_qkv,
     w_dense,
     w_up,
@@ -116,8 +129,16 @@
     attended,
     dense,
     down,
+    full,
+    sums,
+    sums_recv,
+    small_sem,
     load_sem,
     self_sem,
+    gssem,
+    grsem,
+    mssem,
+    mrsem,
     ssem,
     rsem,
     lssem,
@@ -131,7 +152,7 @@
     seq = lax.axis_index("seq")
     head = lax.axis_index("head")
     me = head * seqs + seq
-    rows, width_here = tokens_ref.shape
+    rows, width_here = tokens_hbm.shape
     half = width_here // 2
     heads_here = width_here // HD
     cells = seqs * BLOCK
@@ -147,20 +168,40 @@
         pltpu.make_async_copy(src, dst, load_sem.at[i])
         for i, (src, dst) in enumerate(
             [
+                (w_up_hbm, w_up),
+                (w_down_hbm, w_down),
                 (w_qkv_hbm.at[0], w_qkv.at[0]),
                 (kl_hbm, kl),
+                (vl_hbm, vl),
                 (w_qkv_hbm.at[1], w_qkv.at[1]),
                 (w_qkv_hbm.at[2], w_qkv.at[2]),
-                (vl_hbm, vl),
-                (w_up_hbm, w_up),
-                (w_down_hbm, w_down),
                 (ks_hbm, ks),
                 (vs_hbm, vs),
                 (w_dense_hbm, w_dense),
             ]
         )
     ]
-    load_q, load_kl, load_k, load_v, load_vl, load_up, load_down, load_ks, load_vs, load_d = loads
+    load_up, load_down, load_q, load_kl, load_vl, load_k, load_v, load_ks, load_vs, load_d = loads
+    smalls = [
+        pltpu.make_async_copy(src, dst, small_sem.at[i])
+        for i, (src, dst) in enumerate(
+            [
+                (tokens_hbm, tokens_ref),
+                (slots_hbm, slots_row_ref),
+                (lengths_hbm, lengths_ref),
+                (pieces_hbm, pieces_ref),
+                (freq_hbm, freq_ref),
+                (ln1_gain_hbm, ln1_gain),
+                (ln1_shift_hbm, ln1_shift),
+                (ln2_gain_hbm, ln2_gain),
+                (ln2_shift_hbm, ln2_shift),
+                (b_qkv_hbm, b_qkv),
+                (b_dense_hbm, b_dense),
+                (b_down_hbm, b_down),
+                (b_up_hbm, b_up),
+            ]
+        )
+    ]
 
     barrier = pltpu.get_barrier_semaphore()
 
@@ -171,8 +212,10 @@
         return carry
 
     lax.fori_loop(1, total, hello, 0)
-    for load in loads:
+    for load in smalls + loads:
         load.start()
+    for load in smalls:
+        load.wait()
 
     slots_row = slots_row_ref[...]
     row_ids = iota((rows, 1), 0)
@@ -181,7 +224,7 @@
     position = total_of(jnp.where(slots_row == home_ids, lanes_all, 0), 1)
     my_req = total_of(jnp.where(lanes_all == home_ids, slots_row, 0), 1)
     my_len = total_of(jnp.where(lanes_all == my_req, lengths_ref[...], 0), 1)
-    req_row = slots_ref[pl.ds(seq, 1), :]
+    req_row = total_of(jnp.where(row_ids == iota((rows, rows), 1), my_req, 0), 0)
     group = iota((rows, seqs), 1)
     in_owner = (position >= group * rows) & (position < (group + 1) * rows)
     in_home = (my_req >= group * rows) & (my_req < (group + 1) * rows)
@@ -213,6 +256,32 @@
 
     pl.semaphore_wait(barrier, total - 1)
 
+    def at_band(ref, index):
+        return ref.at[pl.ds(pl.multiple_of(index * rows, rows), rows)]
+
+    def band_copy(src, dst, source, target, send_sems, recv_sems):
+        return pltpu.make_async_remote_copy(
+            src_ref=src,
+            dst_ref=at_band(dst, source),
+            send_sem=send_sems.at[target],
+            recv_sem=recv_sems.at[source],
+            device_id=(seq, target),
+            device_id_type=MESH,
+        )
+
+    def full_copy(target, source):
+        return band_copy(tokens_ref, full, source, target, gssem, grsem)
+
+    def sums_copy(target, source):
+        return band_copy(at_band(sums, target), sums_recv, source, target, mssem, mrsem)
+
+    peers = [lax.rem(head + k, heads) for k in range(1, heads)]
+    sources = [lax.rem(head + heads - k, heads) for k in range(1, heads)]
+    for peer in peers:
+        full_copy(peer, head).start()
+    own_full = pltpu.make_async_copy(tokens_ref, at_band(full, head), self_sem.at[4])
+    own_full.start()
+
     def rows_copy(target, source):
         return pltpu.make_async_remote_copy(
             src_ref=at_block(pack, lax.rem(target, seqs)),
@@ -283,6 +352,22 @@
             + pltpu.roll(values, width_here - ROT // 2, 1) * sine_a[:n]
             + pltpu.roll(values, ROT // 2, 1) * sine_b[:n]
         )
+
+    own_full.wait()
+    for source in sources:
+        full_copy(head, source).wait_recv()
+    at_home = jnp.concatenate([full[h * rows : (h + 1) * rows, :] for h in range(heads)], axis=1)
+    x2[...] = layer_norm(at_home.astype(F32), ln2_gain[...], ln2_shift[...]).astype(BF16)
+    load_up.wait()
+    matmul_into(up, x2, w_up, TILE)
+    before = up[...] + b_up[...]
+    hidden[...] = (0.5 * before * (1.0 + lax.erf(before * (0.5**0.5)))).astype(BF16)
+    load_down.wait()
+    matmul_into(down, hidden, w_down, TILE)
+    for h in range(heads):
+        sums[h * rows : (h + 1) * rows, :] = down[
+            :, h * width_here : (h + 1) * width_here
+        ].astype(BF16)
 
     own_rows.wait()
 
@@ -312,7 +397,11 @@
         [jnp.concatenate(columns, axis=1), jnp.concatenate(long_columns, axis=1)], axis=0
     )
     x1[...] = layer_norm(resident, ln1_gain[...], ln1_shift[...]).astype(BF16)
-    x2[...] = layer_norm(resident[:rows], ln2_gain[...], ln2_shift[...]).astype(BF16)
+
+    for peer in peers:
+        sums_copy(peer, head).start()
+    own_sums = pltpu.make_async_copy(at_band(sums, head), at_band(sums_recv, head), self_sem.at[5])
+    own_sums.start()
 
     scale = HD ** (-0.5)
     load_q.wait()
@@ -367,13 +456,6 @@
     new_value = (qkv[2][:rows] + b_qkv[2:3, :]).astype(BF16).astype(F32)
     product = query.astype(F32) * new_key.astype(F32)
 
-    load_up.wait()
-    matmul_into(up, x2, w_up, TILE)
-    before = up[...] + b_up[...]
-    hidden[...] = (0.5 * before * (1.0 + lax.erf(before * (0.5**0.5)))).astype(BF16)
-    load_down.wait()
-    matmul_into(down, hidden, w_down, TILE)
-
     lane_q = iota((rows, width_here), 1)
     query32 = query.astype(F32)
     split = jnp.concatenate(
@@ -445,8 +527,8 @@
         cols = slice(h * width_here, h * width_here + half)
         rest = slice(h * width_here + half, (h + 1) * width_here)
         back[h * cells : (h + 1) * cells, :] = (
-            dot(give_lo, (dense[:, cols] + down[:, cols]).astype(BF16))
-            + dot(give_hi, (dense[:, rest] + down[:, rest]).astype(BF16))
+            dot(give_lo, dense[:, cols].astype(BF16))
+            + dot(give_hi, dense[:, rest].astype(BF16))
         ).astype(BF16)
 
     def back_copy(target, source):
@@ -489,6 +571,15 @@
         lax.fori_loop(1, total, sent_long, 0)
 
     own_back.wait()
+    own_sums.wait()
+    for peer in peers:
+        full_copy(peer, head).wait_send()
+        sums_copy(peer, head).wait_send()
+    settled = tokens_ref[...].astype(F32) + b_dense[...] + b_down[...]
+    for source in sources:
+        sums_copy(head, source).wait_recv()
+    for h in range(heads):
+        settled = settled + sums_recv[h * rows : (h + 1) * rows, :].astype(F32)
 
     def back_arrive(k, carry):
         back_copy(lax.rem(me + k, total), me).wait_send()
@@ -503,8 +594,7 @@
         block = back_recv[h * cells : (h + 1) * cells, :]
         low = low + dot(take_lo, block)
         high = high + dot(take_hi, block)
-    finished = tokens_ref[...].astype(F32) + jnp.concatenate([low, high], axis=1)
-    out_ref[...] = (finished + b_out[0:1, :] + b_out[1:2, :]).astype(BF16)
+    out_ref[...] = (settled + jnp.concatenate([low, high], axis=1)).astype(BF16)
 
 
 TILE = 512
@@ -548,9 +638,22 @@
     return pl.pallas_call(
         functools.partial(layer_kernel, seqs, heads),
         out_shape=jax.ShapeDtypeStruct((rows, width_here), BF16),
-        in_specs=[vmem] * 13 + [hbm] * 8,
+        in_specs=[hbm] * 21,
         out_specs=vmem,
         scratch_shapes=[
+            pltpu.VMEM((rows, width_here), BF16),
+            pltpu.VMEM((1, seqs * rows), jnp.int32),
+            pltpu.VMEM((1, seqs * rows), jnp.int32),
+            pltpu.VMEM((1, seqs), jnp.int32),
+            pltpu.VMEM((1, 128), F32),
+            pltpu.VMEM((1, width), F32),
+            pltpu.VMEM((1, width), F32),
+            pltpu.VMEM((1, width), F32),
+            pltpu.VMEM((1, width), F32),
+            pltpu.VMEM((3, width_here), F32),
+            pltpu.VMEM((1, width_here), F32),
+            pltpu.VMEM((1, width_here), F32),
+            pltpu.VMEM((1, units), F32),
             pltpu.VMEM((3, width, width_here), BF16),
             pltpu.VMEM((width_here, width), BF16),
             pltpu.VMEM((width, units), BF16),
@@ -575,8 +678,16 @@
             pltpu.VMEM((rows, width_here), BF16),
             pltpu.VMEM((rows, width), F32),
             pltpu.VMEM((rows, width), F32),
+            pltpu.VMEM((heads * rows, width_here), BF16),
+            pltpu.VMEM((heads * rows, width_here), BF16),
+            pltpu.VMEM((heads * rows, width_here), BF16),
+            dma((13,)),
             dma((10,)),
-            dma((4,)),
+            dma((6,)),
+            dma((heads,)),
+            dma((heads,)),
+            dma((heads,)),
+            dma((heads,)),
             dma((total,)),
             dma((total,)),
             dma((total,)),
@@ -592,18 +703,18 @@
         name="layer",
     )(
         tokens,
+        slot_request[None],
+        lengths[None],
+        piece_map[None],
+        freq,
         ln1_gain[None],
         ln1_shift[None],
         ln2_gain[None],
         ln2_shift[None],
         b_qkv,
-        jnp.stack([b_dense, b_down]),
+        b_dense[None],
+        b_down[None],
         b_up[None],
-        lengths[None],
-        slot_request[None],
-        slot_request.reshape(seqs, rows),
-        piece_map[None],
-        freq,
         jnp.transpose(w_qkv, (1, 0, 2)),
         w_dense,
         w_up,

time: 46 us -> 51.2 us (1.11)
  Pallas kernels: 41.6 us -> 49.6 us
  local copies, waits for them, and re-layouts: 2.82 us -> 1.47 us
  other arithmetic: 1.31 us -> 0 us
    pallas_call x1, Pallas kernels: 41.6 us -> 49.6 us  [local(): pl.pallas_call(functools.partial(layer_kernel, seqs, heads), out_shape=ja...]
    reshape x1 -> x0, local copies, waits for them, and re-layouts: 1.35 us -> none  [local(): slot_request.reshape(seqs, rows)]
    another operation x1 -> x0, other arithmetic: 1.31 us -> none  [local(): jnp.stack([b_dense, b_down])]
where the time goes in v3:
time: 51.2 us; the launch traced here: 51 us
  Pallas kernels  49.6 us (97%)
  local copies, waits for them, and re-layouts  1.47 us (3%)
    pallas_call x1, Pallas kernels, local(): pl.pallas_call(functools.partial(layer_kernel, seqs, heads), out_shape=ja...  49.6 us
    unnamed x1, local copies, waits for them, and re-layouts  1.47 us

profile of v3, /device:TPU:0, one launch (start us, length us, event | category | flops | bytes accessed | tf_op | source)
XLA Modules:
  0.0 51.0 jit_solution(7178895634751382226)
XLA Ops:
  0.0 49.6 %layer.1 = bf16[32,1024]{1,0:T(8,128)(2,1)} custom-call(bf16[32,1024]{1,0:T(8,128)(2,1)} %tokens_hbm.1, s32[1,512]{1,0:T(1,128)} %bitcast.23, s32[1,512]{1,0:T(1,128)} %bitcast.24, s32[1,16]{1,0:T(1,128)} %bitcast.25, f32[1,128]{1,0:T(1,128)} %constant.2.clone.freq_hbm, f32[1,2048]{1,0:T(1,128)} %bitcast.16, f32[1,2048]{1,0:T(1,128)} %bitcast.17, ...), custom_call_target="tpu_custom_call" | custom-call | tf_op jit(solution)/shard_map/layer/pallas_call | solution.py:638
  49.6 1.5 %copy.23 = bf16[32,1024]{1,0:T(8,128)(2,1)} copy(bf16[32,1024]{1,0:T(8,128)(2,1)} %layer.1) | data formatting | bytes 131072

commit v4 on v3

--- a/solution.py
+++ b/solution.py
@@ -59,6 +59,8 @@
 
 
 def matmul_into(out_ref, x_ref, w_ref, tile):
+    tile = min(tile, w_ref.shape[1])
+
     def step(i, carry):
         cols = pl.ds(pl.multiple_of(i * tile, tile), tile)
         out_ref[:, cols] = dot(x_ref[...], w_ref[:, cols])
@@ -70,28 +72,6 @@
 def layer_kernel(
     seqs,
     heads,
-    tokens_hbm,
-    slots_hbm,
-    lengths_hbm,
-    pieces_hbm,
-    freq_hbm,
-    ln1_gain_hbm,
-    ln1_shift_hbm,
-    ln2_gain_hbm,
-    ln2_shift_hbm,
-    b_qkv_hbm,
-    b_dense_hbm,
-    b_down_hbm,
-    b_up_hbm,
-    w_qkv_hbm,
-    w_dense_hbm,
-    w_up_hbm,
-    w_down_hbm,
-    ks_hbm,
-    vs_hbm,
-    kl_hbm,
-    vl_hbm,
-    out_ref,
     tokens_ref,
     slots_row_ref,
     lengths_ref,
@@ -105,6 +85,15 @@
     b_dense,
     b_down,
     b_up,
+    w_qkv_hbm,
+    w_dense_hbm,
+    w_up_hbm,
+    w_down_hbm,
+    ks_hbm,
+    vs_hbm,
+    kl_hbm,
+    vl_hbm,
+    out_ref,
     w_qkv,
     w_dense,
     w_up,
@@ -132,7 +121,6 @@
     full,
     sums,
     sums_recv,
-    small_sem,
     load_sem,
     self_sem,
     gssem,
@@ -152,7 +140,7 @@
     seq = lax.axis_index("seq")
     head = lax.axis_index("head")
     me = head * seqs + seq
-    rows, width_here = tokens_hbm.shape
+    rows, width_here = tokens_ref.shape
     half = width_here // 2
     heads_here = width_here // HD
     cells = seqs * BLOCK
@@ -182,27 +170,6 @@
         )
     ]
     load_up, load_down, load_q, load_kl, load_vl, load_k, load_v, load_ks, load_vs, load_d = loads
-    smalls = [
-        pltpu.make_async_copy(src, dst, small_sem.at[i])
-        for i, (src, dst) in enumerate(
-            [
-                (tokens_hbm, tokens_ref),
-                (slots_hbm, slots_row_ref),
-                (lengths_hbm, lengths_ref),
-                (pieces_hbm, pieces_ref),
-                (freq_hbm, freq_ref),
-                (ln1_gain_hbm, ln1_gain),
-                (ln1_shift_hbm, ln1_shift),
-                (ln2_gain_hbm, ln2_gain),
-                (ln2_shift_hbm, ln2_shift),
-                (b_qkv_hbm, b_qkv),
-                (b_dense_hbm, b_dense),
-                (b_down_hbm, b_down),
-                (b_up_hbm, b_up),
-            ]
-        )
-    ]
-
     barrier = pltpu.get_barrier_semaphore()
 
     def hello(k, carry):
@@ -212,10 +179,8 @@
         return carry
 
     lax.fori_loop(1, total, hello, 0)
-    for load in smalls + loads:
+    for load in loads:
         load.start()
-    for load in smalls:
-        load.wait()
 
     slots_row = slots_row_ref[...]
     row_ids = iota((rows, 1), 0)
@@ -597,7 +562,7 @@
     out_ref[...] = (settled + jnp.concatenate([low, high], axis=1)).astype(BF16)
 
 
-TILE = 512
+TILE = 1024
 
 
 def local(
@@ -638,22 +603,9 @@
     return pl.pallas_call(
         functools.partial(layer_kernel, seqs, heads),
         out_shape=jax.ShapeDtypeStruct((rows, width_here), BF16),
-        in_specs=[hbm] * 21,
+        in_specs=[vmem] * 13 + [hbm] * 8,
         out_specs=vmem,
         scratch_shapes=[
-            pltpu.VMEM((rows, width_here), BF16),
-            pltpu.VMEM((1, seqs * rows), jnp.int32),
-            pltpu.VMEM((1, seqs * rows), jnp.int32),
-            pltpu.VMEM((1, seqs), jnp.int32),
-            pltpu.VMEM((1, 128), F32),
-            pltpu.VMEM((1, width), F32),
-            pltpu.VMEM((1, width), F32),
-            pltpu.VMEM((1, width), F32),
-            pltpu.VMEM((1, width), F32),
-            pltpu.VMEM((3, width_here), F32),
-            pltpu.VMEM((1, width_here), F32),
-            pltpu.VMEM((1, width_here), F32),
-            pltpu.VMEM((1, units), F32),
             pltpu.VMEM((3, width, width_here), BF16),
             pltpu.VMEM((width_here, width), BF16),
             pltpu.VMEM((width, units), BF16),
@@ -681,7 +633,6 @@
             pltpu.VMEM((heads * rows, width_here), BF16),
             pltpu.VMEM((heads * rows, width_here), BF16),
             pltpu.VMEM((heads * rows, width_here), BF16),
-            dma((13,)),
             dma((10,)),
             dma((6,)),
             dma((heads,)),

time: 51.2 us -> 40.5 us (0.79)
  Pallas kernels: 49.6 us -> 38.8 us
    pallas_call x1, Pallas kernels: 49.6 us -> 38.8 us  [local(): pl.pallas_call(functools.partial(layer_kernel, seqs, heads), out_shape=ja...]
where the time goes in v4:
time: 40.5 us; the launch traced here: 40.3 us
  Pallas kernels  38.8 us (96%)
  local copies, waits for them, and re-layouts  1.47 us (4%)
    pallas_call x1, Pallas kernels, local(): pl.pallas_call(functools.partial(layer_kernel, seqs, heads), out_shape=ja...  38.8 us
    unnamed x1, local copies, waits for them, and re-layouts  1.47 us

profile of v4, /device:TPU:0, one launch (start us, length us, event | category | flops | bytes accessed | tf_op | source)
XLA Modules:
  0.0 40.3 jit_solution(348417879880049055)
XLA Ops:
  0.0 38.8 %layer.1 = bf16[32,1024]{1,0:T(8,128)(2,1)} custom-call(bf16[32,1024]{1,0:T(8,128)(2,1)} %tokens_ref.1, s32[1,512]{1,0:T(1,128)} %bitcast.23, s32[1,512]{1,0:T(1,128)} %bitcast.24, s32[1,16]{1,0:T(1,128)} %bitcast.25, f32[1,128]{1,0:T(1,128)} %constant.2.clone.freq_ref, f32[1,2048]{1,0:T(1,128)} %bitcast.16, f32[1,2048]{1,0:T(1,128)} %bitcast.17, ...), custom_call_target="tpu_custom_call" | custom-call | tf_op jit(solution)/shard_map/layer/pallas_call | solution.py:603
  38.8 1.5 %copy.23 = bf16[32,1024]{1,0:T(8,128)(2,1)} copy(bf16[32,1024]{1,0:T(8,128)(2,1)} %layer.1) | data formatting | bytes 131072
